TPU v7x, 128 devices: a whole 4x4x4 slice. The times are simulated.
128 devices in a mesh: seq: 32 (over y, x, core), hid: 4 (over z).
Axes of the slice: x: 4, y: 4, z: 4, core: 2. Of those that a mesh axis runs over, the one named last changes fastest.
Arguments:
- patches: bfloat16 [12288, 3200], P('seq'), may hold values from -6 to 6
- norm_gain: float32 [3200], replicated, may hold values from 0.5 to 8
- query_weight: bfloat16 [3200, 2048], P(None, 'hid'), may hold values from -0.109375 to 0.109375
- key_weight: bfloat16 [3200, 2048], P(None, 'hid'), may hold values from -0.7424621 to 0.7424621
- value_weight: bfloat16 [3200, 2048], P(None, 'hid'), may hold values from -0.109375 to 0.109375
- out_weight: bfloat16 [2048, 3200], P('hid'), may hold values from -0.125 to 0.125
- layer_scale: float32 [3200], replicated, may hold values from 0.3 to 1.5
- merge_gain: float32 [12800], P('hid'), may hold values from 0.5 to 1.5
- merge_bias: float32 [12800], P('hid'), may hold values from -3 to 3
- proj_weight: bfloat16 [12800, 6144], P('hid', 'seq'), may hold values from -0.0546875 to 0.0546875
- proj_bias: float32 [6144], P('seq'), may hold values from -3 to 3
- text_rows: bfloat16 [512, 6144], P(None, 'seq'), may hold values from -6 to 6
- stream_gain: float32 [6144], P('hid'), may hold values from 0.5 to 1.5
- tile_counts: int32 [3], replicated, may hold values from 1 to 7, as said below
- image_slots: int32 [3072], replicated, may hold values from 0 to 3583, as said below
- text_slots: int32 [512], replicated, may hold values from 0 to 3583, as said below
Outputs:
- stream: bfloat16 [3584, 6144], P('seq', 'hid')
- normed: bfloat16 [3584, 6144], P('seq', 'hid')
Inputs may be any that keep to these rules, and one draw needn't show every extreme that they name: `tile_counts`: the tile counts sum to 12; the largest is exactly 7. `image_slots`: image slots and text slots together name every stream position once; each image's rows lie in order at consecutive positions. `text_slots`: see image_slots; text slots increase.
All inputs are finite; a program needn't handle non-finite values.
Results may differ from a plain program's by a relative error of at most 0.022.
The roundings to bfloat16 on the way count: a program that leaves them out, or rounds other values in their place, can miss the bound.
Values may be sent and summed in bfloat16 or wider, within the bound.
No kernel may reach another device: no remote copies, remote signals or barrier semaphores. Data moves between devices by JAX's collectives and lax.ppermute only.
A program may use at most 192 MiB of HBM per device.

v0:
```python
import jax
import jax.numpy as jnp
from jax import lax
from jax.sharding import PartitionSpec as P

HD = 128
SIDE = 32


def image_of(index_rows, tile_counts):
    bounds = jnp.cumsum(tile_counts) * (SIDE * SIDE)
    return jnp.sum((index_rows[:, None] >= bounds[None, :]).astype(jnp.int32), axis=1)


def shuffle_rows(values):
    row_count, width = values.shape
    grouped = values.reshape(row_count // (2 * SIDE), 2, SIDE // 2, 2, width)
    return grouped.transpose(0, 2, 4, 1, 3).reshape(row_count // 4, 4 * width)


def per_device(
    patches,
    norm_gain,
    query_weight,
    key_weight,
    value_weight,
    out_weight,
    layer_scale,
    merge_gain,
    merge_bias,
    proj_weight,
    proj_bias,
    text_rows,
    stream_gain,
    tile_counts,
    image_slots,
    text_slots,
):
    seq_index = lax.axis_index("seq")
    hid_index = lax.axis_index("hid")
    local_rows = patches.shape[0]
    local_heads = query_weight.shape[1] // HD
    tokens_f = patches.astype(jnp.float32)
    normed_in = (
        tokens_f * lax.rsqrt(jnp.mean(tokens_f * tokens_f, -1, keepdims=True) + 1e-06) * norm_gain
    ).astype(jnp.bfloat16)
    queries = (
        jnp.dot(normed_in, query_weight, preferred_element_type=jnp.float32) * HD ** (-0.5)
    ).astype(jnp.bfloat16)
    key_rows = jnp.dot(normed_in, key_weight, preferred_element_type=jnp.float32).astype(
        jnp.bfloat16
    )
    value_rows = jnp.dot(normed_in, value_weight, preferred_element_type=jnp.float32).astype(
        jnp.bfloat16
    )
    query_heads = queries.reshape(local_rows, local_heads, HD)
    query_ids = image_of(
        seq_index * local_rows + jnp.arange(local_rows, dtype=jnp.int32), tile_counts
    )

    def fold_block(state_now, key_block, value_block, block_start):
        maxima, totals, accumulated = state_now
        row_count = key_block.shape[0]
        key_heads = key_block.reshape(row_count, local_heads, HD)
        value_heads = value_block.reshape(row_count, local_heads, HD)
        scores = jnp.einsum(
            "qhd,khd->hqk", query_heads, key_heads, preferred_element_type=jnp.float32
        )
        key_ids = image_of(block_start + jnp.arange(row_count, dtype=jnp.int32), tile_counts)
        same_image = (query_ids[:, None] == key_ids[None, :])[None]
        scores = jnp.where(same_image, scores, jnp.float32(-1e30))
        new_max = jnp.maximum(maxima, jnp.max(scores, axis=-1))
        factor = jnp.exp(maxima - new_max)
        weights = jnp.where(same_image, jnp.exp(scores - new_max[..., None]), jnp.float32(0.0))
        totals = totals * factor + jnp.sum(weights, axis=-1)
        update = jnp.einsum(
            "hqk,khd->hqd",
            weights.astype(jnp.bfloat16),
            value_heads,
            preferred_element_type=jnp.float32,
        )
        accumulated = accumulated * factor[..., None] + update
        return (new_max, totals, accumulated)

    start_state = (
        jnp.full((local_heads, local_rows), -1e30, jnp.float32),
        jnp.zeros((local_heads, local_rows), jnp.float32),
        jnp.zeros((local_heads, local_rows, HD), jnp.float32),
    )
    key_piece = lax.all_gather(key_rows, "seq", axis=0, tiled=True)
    value_piece = lax.all_gather(value_rows, "seq", axis=0, tiled=True)
    row_count = key_piece.shape[0]
    block_rows = 512
    steps_count = row_count // block_rows
    key_blocks = key_piece.reshape(steps_count, block_rows, key_piece.shape[1])
    value_blocks = value_piece.reshape(steps_count, block_rows, value_piece.shape[1])

    def step_fn(state_in, inputs):
        key_block, value_block, index_now = inputs
        return (fold_block(state_in, key_block, value_block, index_now * block_rows), None)

    result, unused = lax.scan(
        step_fn, start_state, (key_blocks, value_blocks, jnp.arange(steps_count, dtype=jnp.int32))
    )
    maxima, totals, accumulated = result
    attended = (accumulated / totals[..., None]).astype(jnp.bfloat16)
    attended = attended.transpose(1, 0, 2).reshape(local_rows, local_heads * HD)
    branch_part = jnp.dot(attended, out_weight, preferred_element_type=jnp.float32)
    branch = lax.psum(branch_part.astype(jnp.bfloat16), "hid").astype(jnp.float32)
    merged = shuffle_rows(tokens_f + layer_scale * branch)
    mean_row = jnp.mean(merged, -1, keepdims=True)
    var_row = jnp.mean(merged * merged, -1, keepdims=True) - mean_row * mean_row
    block_width = merged.shape[1] // lax.axis_size("hid")
    merged_block = lax.dynamic_slice_in_dim(merged, hid_index * block_width, block_width, 1)
    merged_normed = (
        (merged_block - mean_row) * lax.rsqrt(var_row + 1e-05) * merge_gain + merge_bias
    ).astype(jnp.bfloat16)
    partial_proj = jnp.dot(
        lax.all_gather(merged_normed, "seq", axis=0, tiled=True),
        proj_weight,
        preferred_element_type=jnp.float32,
    )
    stream_size = image_slots.shape[0] + text_slots.shape[0]
    summed = lax.psum(partial_proj.astype(jnp.bfloat16), "hid").astype(jnp.float32)
    image_rows = jax.nn.gelu(summed + proj_bias, approximate=False).astype(jnp.bfloat16)
    stream_cols = (
        jnp.zeros((stream_size, image_rows.shape[1]), jnp.bfloat16)
        .at[image_slots]
        .set(image_rows)
        .at[text_slots]
        .set(text_rows)
    )
    stream_full = lax.all_to_all(stream_cols, "seq", split_axis=0, concat_axis=1, tiled=True)
    stream_f = stream_full.astype(jnp.float32)
    inverse_rms = lax.rsqrt(jnp.mean(stream_f * stream_f, -1, keepdims=True) + 1e-05)
    out_width = stream_full.shape[1] // lax.axis_size("hid")
    stream_share = lax.dynamic_slice_in_dim(stream_full, hid_index * out_width, out_width, 1)
    normed_share = (stream_share.astype(jnp.float32) * inverse_rms * stream_gain).astype(
        jnp.bfloat16
    )
    return (stream_share, normed_share)


def solution(mesh):
    return jax.shard_map(
        per_device,
        mesh=mesh,
        in_specs=(
            P("seq", None),
            P(),
            P(None, "hid"),
            P(None, "hid"),
            P(None, "hid"),
            P("hid", None),
            P(),
            P("hid"),
            P("hid"),
            P("hid", "seq"),
            P("seq"),
            P(None, "seq"),
            P("hid"),
            P(),
            P(),
            P(),
        ),
        out_specs=(P("seq", "hid"), P("seq", "hid")),
        check_vma=False,
    )
```

profile of v0, /device:TPU:0, one launch (start us, length us, event | category | flops | bytes accessed | tf_op | source)
XLA Modules:
  0.0 976.0 jit_solution(10442808038477700343)
XLA Ops:
  14.1 5.0 convolution_convert_fusion.2
  24.6 54.9 %all-gather.4.cloned.1.call-done = bf16[12288,512]{1,0:T(8,128)(2,1)} async-done(((bf16[384,512]{1,0:T(8,128)(2,1)}), bf16[12288,512]{1,0:T(8,128)(2,1)}) %all-gather.4.cloned.1.call-update) | async-done | bytes 12582928 | tf_op jit(solution)/shard_map/all_gather | solution.py:90
  79.5 64.6 %all-gather.6.cloned.1.call-done = bf16[12288,512]{1,0:T(8,128)(2,1)} async-done(((bf16[384,512]{1,0:T(8,128)(2,1)}), bf16[12288,512]{1,0:T(8,128)(2,1)}) %all-gather.6.cloned.1.call-update) | async-done | bytes 12582928 | tf_op jit(solution)/shard_map/all_gather | solution.py:91
  144.1 443.7 %while.17 = (s32[]{:T(128)}, f32[4,384]{1,0:T(4,128)S(1)}, f32[4,384]{1,0:T(4,128)S(1)}, f32[4,384,128]{2,1,0:T(8,128)}, s32[384]{0:T(512)S(1)}, /*index=5*/s32[...) while((s32[]{:T(128)}, f32[4,384]{1,0:T(4,128)S(1)}, ...), condition=%wide.region_7.8_spmd.clone, body=%wide.region_3.7_spmd.clone.sunk | while | flops 411316224 | bytes 17540812 | solution.py:102
  176.6 4.3 fusion.63
  213.6 4.3 fusion.63
  232.1 4.3 fusion.63
  361.6 4.3 fusion.63
  380.1 4.3 fusion.63
  528.1 4.3 fusion.63
  565.1 4.3 fusion.63
  594.5 64.3 %all-reduce.3.cloned.1.call-done = bf16[384,3200]{1,0:T(8,128)(2,1)} async-done(((bf16[384,3200]{1,0:T(8,128)(2,1)}), bf16[384,3200]{1,0:T(8,128)(2,1)}) %all-reduce.3.cloned.1.call-update) | async-done | bytes 2457616 | tf_op jit(solution)/shard_map/psum | solution.py:109
  658.9 4.5 convert_add_fusion
  663.4 6.8 reshape.161
  670.2 39.8 %copy.71 = f32[6,2,16,2,3200]{2,0,3,1,4:T(8,128)} copy(f32[6,2,16,2,3200]{4,3,2,1,0:T(2,128)} %reshape.161) | data formatting | bytes 9830400 | tf_op jit(solution)/shard_map/reshape | solution.py:17
  709.9 17.3 %bitcast_reduce_fusion = (f32[6,16]{1,0:T(8,128)S(1)}, f32[6,16]{1,0:T(8,128)S(1)}) fusion(f32[6,2,16,2,3200]{2,0,3,1,4:T(8,128)} %copy.71), kind=kLoop, calls=%fused_computation.81 | loop fusion | flops 3686208 | bytes 4915968 | tf_op jit(solution)/shard_map/reduce_sum | solution.py:111
  727.4 31.2 %reshape.162 = f32[96,12800]{0,1:T(8,128)} reshape(f32[6,16,3200,2,2]{1,0,4,3,2:T(8,128)} %bitcast.71) | data formatting | bytes 9830400 | tf_op jit(solution)/shard_map/reshape | solution.py:18
  761.8 78.9 %all-gather.8.cloned.1.call-done = bf16[3072,3200]{1,0:T(8,128)(2,1)} async-done(((bf16[96,3200]{1,0:T(8,128)(2,1)}), bf16[3072,3200]{1,0:T(8,128)(2,1)}) %all-gather.8.cloned.1.call-update) | async-done | bytes 19660816 | tf_op jit(solution)/shard_map/all_gather | solution.py:119
  840.7 14.4 %convolution_convert_fusion.1 = bf16[3072,192]{0,1:T(8,128)(2,1)} fusion(bf16[3072,3200]{1,0:T(8,128)(2,1)} %all-gather.8.cloned.1.call-done, bf16[3200,192]{0,1:T(8,128)(2,1)} %param.27), kind=kOutput, calls=%fused_computation.34 | convolution fusion | flops 3775463424 | bytes 22069248 | tf_op jit(solution)/shard_map/dot_general | solution.py:118
  855.3 46.3 %all-reduce.5.cloned.1.call-done = bf16[3072,192]{0,1:T(8,128)(2,1)} async-done(((bf16[3072,192]{0,1:T(8,128)(2,1)}), bf16[3072,192]{0,1:T(8,128)(2,1)}) %all-reduce.5.cloned.1.call-update) | async-done | bytes 1179664 | tf_op jit(solution)/shard_map/psum | solution.py:124
  901.6 6.4 fusion.20
  909.6 14.5 %scatter_custom_fusion = bf16[3584,192]{1,0:T(8,128)(2,1)S(1)} fusion(s32[3072]{0:T(1024)S(1)} %compare_select_fusion, bf16[3072,192]{1,0:T(8,128)(2,1)} %copy.73, bf16[]{:T(256)} %constant.65.clone.1), kind=kCustom, calls=%fused_computation.64 | custom fusion | bytes 1376768 | tf_op jit(solution)/shard_map/scatter | solution.py:129
  930.0 7.3 all-to-all-start
  937.4 23.9 %all-to-all-done = bf16[32,112,192]{1,2,0:T(8,128)(2,1)} async-done(((bf16[32,112,192]{1,2,0:T(8,128)(2,1)}), bf16[32,112,192]{1,2,0:T(8,128)(2,1)}, u32[]{:S(2)}, u32[]{:S(2)}) %all-to-all-start) | async-done | bytes 1376288 | tf_op jit(solution)/shard_map/all_to_all | solution.py:133
  (401 shorter events, 435.6 us)
Async XLA Ops:
  7.2 584.1 %copy-start = (bf16[512,3200]{1,0:T(8,128)(2,1)S(1)}, bf16[512,3200]{1,0:T(8,128)(2,1)}, u32[]{:S(2)}) copy-start(bf16[512,3200]{1,0:T(8,128)(2,1)} %param.23) | copy-start | bytes 9830404
  7.2 72.3 %all-gather.4.cloned.1.call-start = ((), (), s32[]{:S(2)}) async-start(), calls=%async_computation.1 | async-start | bytes 12976128 | tf_op jit(solution)/shard_map/all_gather | solution.py:90
  7.2 2.6 copy-start.2
  9.8 4.3 copy-start.12
  14.1 130.0 %all-gather.6.cloned.1.call-start = ((), (), s32[]{:S(2)}) async-start(), calls=%async_computation.2 | async-start | bytes 12976128 | tf_op jit(solution)/shard_map/all_gather | solution.py:91
  19.2 639.7 %all-reduce.3.cloned.1.call-start = ((), (), s32[]{:S(2)}) async-start(), calls=%async_computation.3 | async-start | bytes 4915200 | tf_op jit(solution)/shard_map/psum | solution.py:109
  19.2 5.1 copy-start.13
  591.3 67.6 %copy-start.5 = (f32[3200]{0:T(1024)S(1)}, f32[3200]{0:T(1024)}, u32[]{:S(2)}) copy-start(f32[3200]{0:T(1024)} %param.24) | copy-start | bytes 38404
  594.3 64.6 %copy-start.3 = (bf16[384,3200]{1,0:T(8,128)(2,1)S(1)}, bf16[384,3200]{1,0:T(8,128)(2,1)}, u32[]{:S(2)}) copy-start(bf16[384,3200]{1,0:T(8,128)(2,1)} %param.18) | copy-start | bytes 7372804
  594.3 246.4 %all-gather.8.cloned.1.call-start = ((), (), s32[]{:S(2)}) async-start(), calls=%async_computation.4 | async-start | bytes 20275200 | tf_op jit(solution)/shard_map/all_gather | solution.py:119
  758.5 2.1 copy-start.6
  758.5 2.1 copy-start.7
  761.7 93.4 %copy-start.4 = (bf16[512,192]{0,1:T(8,128)(2,1)S(1)}, bf16[512,192]{0,1:T(8,128)(2,1)}, u32[]{:S(2)}) copy-start(bf16[512,192]{0,1:T(8,128)(2,1)} %param.29) | copy-start | bytes 589828
  761.8 93.6 %copy-start.10 = (s32[512]{0:T(512)S(1)}, s32[512]{0:T(512)}, u32[]{:S(2)}) copy-start(s32[512]{0:T(512)} %param.33) | copy-start | bytes 6148
  761.8 93.6 %copy-start.8 = (s32[3072]{0:T(1024)S(1)}, s32[3072]{0:T(1024)}, u32[]{:S(2)}) copy-start(s32[3072]{0:T(1024)} %param.32) | copy-start | bytes 36868
  761.8 139.8 %copy-start.11 = (f32[192]{0:T(256)S(1)}, f32[192]{0:T(256)}, u32[]{:S(2)}) copy-start(f32[192]{0:T(256)} %param.28) | copy-start | bytes 2308
  761.8 139.8 %all-reduce.5.cloned.1.call-start = ((), (), s32[]{:S(2)}) async-start(), calls=%async_computation.5 | async-start | bytes 2359296 | tf_op jit(solution)/shard_map/psum | solution.py:124
  930.0 33.5 %copy-start.9 = (f32[1536]{0:T(1024)S(1)}, f32[1536]{0:T(1024)}, u32[]{:S(2)}) copy-start(f32[1536]{0:T(1024)} %param.30) | copy-start | bytes 18436
  930.0 31.3 %all-to-all-start = ((bf16[32,112,192]{1,2,0:T(8,128)(2,1)}), bf16[32,112,192]{1,2,0:T(8,128)(2,1)}, u32[]{:S(2)}, u32[]{:S(2)}) async-start(bf16[32,112,192]{1,2,0:T(8,128)(2,1)} %copy.76), calls=%async_computation | async-start | bytes 3145728 | tf_op jit(solution)/shard_map/all_to_all | solution.py:133
  937.4 32.1 %copy-start.1 = (bf16[512,3200]{1,0:T(8,128)(2,1)S(1)}, bf16[512,3200]{1,0:T(8,128)(2,1)}, u32[]{:S(2)}) copy-start(bf16[512,3200]{1,0:T(8,128)(2,1)} %param.23) | copy-start | bytes 9830404
Sparse Core Ops, SparseCore 0:
  14.2 65.2 all-gather.3
  81.7 62.3 all-gather.5
  594.4 64.4 all-reduce.2
  761.9 78.7 all-gather.7
  855.3 46.2 all-reduce.4
where the time goes:
time: 982 us; the launch traced here: 976 us
  waiting for transfers between devices  333 us (34%)
  local copies, waits for them, and re-layouts  279 us (28%)
  matrix products  220 us (22%)
  other arithmetic  106 us (11%)
  loops' own time  16.4 us (2%)
  between operations  14 us (1%)
    dynamic_slice x96, local copies, waits for them, and re-layouts, per_device(): lax.scan(step_fn, start_state, (key_blocks, value_blocks, jnp.arange(step...  169 us
    dot_general x24, matrix products, fold_block(): jnp.einsum('hqk,khd->hqd', weights.astype(jnp.bfloat16), value_heads, pre...  102 us
    dot_general x24, matrix products, fold_block(): jnp.einsum('qhd,khd->hqk', query_heads, key_heads, preferred_element_type...  87.1 us
    all_gather x1, waiting for transfers between devices, per_device(): lax.all_gather(merged_normed, 'seq', axis=0, tiled=True)  78.9 us
    all_gather x1, waiting for transfers between devices, per_device(): value_piece = lax.all_gather(value_rows, 'seq', axis=0, tiled=True)  64.6 us
    psum x1, waiting for transfers between devices, per_device(): lax.psum(branch_part.astype(jnp.bfloat16), 'hid').astype(jnp.float32)  64.3 us
    reduce_sum x24, other arithmetic, fold_block(): totals = totals * factor + jnp.sum(weights, axis=-1)  61.6 us
    all_gather x1, waiting for transfers between devices, per_device(): key_piece = lax.all_gather(key_rows, 'seq', axis=0, tiled=True)  54.9 us
  transfers between devices with their start and end apart: 6, of which 6 were waited for; matrix products, arithmetic and copies ran while one was open for 1% of the time, Pallas kernels for 0%

commit v1 on v0

v1 whole, which is shorter than its diff:
```python
import jax
import jax.numpy as jnp
from jax import lax
from jax.experimental import pallas as pl
from jax.experimental.pallas import tpu as pltpu
from jax.sharding import Mesh, PartitionSpec as P

HD = 128
ROWS = 384
MROWS = 96
BF = jnp.bfloat16
F32 = jnp.float32
LIMIT = 60 * 1024 * 1024


def cdot(a, b):
    return jnp.dot(a, b, preferred_element_type=F32)


def shift(value, axis, k):
    return lax.ppermute(value, axis, [(i, (i + k) % 4) for i in range(4)])


def swap(value):
    return lax.ppermute(value, "c", [(0, 1), (1, 0)])


def call(body, out_shape, scratch=(), **kw):
    return pl.pallas_call(
        body,
        out_shape=out_shape,
        scratch_shapes=scratch,
        compiler_params=pltpu.CompilerParams(vmem_limit_bytes=LIMIT),
        **kw,
    )


SMEM = pl.BlockSpec(memory_space=pltpu.SMEM)
VMEM = pl.BlockSpec(memory_space=pltpu.VMEM)
ANY = pl.BlockSpec(memory_space=pl.ANY)


def sub_row_permutation():
    row = lax.broadcasted_iota(jnp.int32, (ROWS, ROWS), 0)
    col = lax.broadcasted_iota(jnp.int32, (ROWS, ROWS), 1)
    sub = (row >= 96).astype(jnp.int32) + (row >= 192).astype(jnp.int32) + (row >= 288).astype(jnp.int32)
    m = row - 96 * sub
    source = (2 * (m >> 4) + (sub >> 1)) * 32 + 2 * (m & 15) + (sub & 1)
    return jnp.where(source == col, 1.0, 0.0).astype(BF)


def qkv_body(s_ref, x_ref, g_ref, wk_ref, wv_ref, wq_ref, kv_ref, q_ref, xn_ref):
    half = pl.program_id(0)

    @pl.when(half == 0)
    def _():
        xf = cdot(sub_row_permutation(), x_ref[...])
        scale = lax.rsqrt(jnp.mean(xf * xf, axis=-1, keepdims=True) + 1e-06)
        xn_ref[...] = (xf * scale * g_ref[...]).astype(BF)

    xn = xn_ref[...]
    keys = cdot(xn, wk_ref[...]).astype(BF)
    values = cdot(xn, wv_ref[...]).astype(BF)
    queries = (cdot(xn, wq_ref[...]) * HD ** (-0.5)).astype(BF)
    for i in range(2):
        slot = (2 * half + i - s_ref[0]) & 3
        part = slice(HD * i, HD * (i + 1))
        kv_ref[slot, :, 0:HD] = keys[:, part]
        kv_ref[slot, :, HD : 2 * HD] = values[:, part]
        q_ref[slot] = queries[:, part]


def project_qkv(y, patches, gain, wk, wv, wq):
    width = patches.shape[1]
    whole = pl.BlockSpec((ROWS, width), lambda j, s: (0, 0))
    weight = pl.BlockSpec((width, 2 * HD), lambda j, s: (0, j))
    return pl.pallas_call(
        qkv_body,
        out_shape=(
            jax.ShapeDtypeStruct((4, ROWS, 2 * HD), BF),
            jax.ShapeDtypeStruct((4, ROWS, HD), BF),
        ),
        grid_spec=pltpu.PrefetchScalarGridSpec(
            num_scalar_prefetch=1,
            grid=(2,),
            in_specs=[whole, pl.BlockSpec((1, width), lambda j, s: (0, 0)), weight, weight, weight],
            out_specs=[
                pl.BlockSpec((4, ROWS, 2 * HD), lambda j, s: (0, 0, 0)),
                pl.BlockSpec((4, ROWS, HD), lambda j, s: (0, 0, 0)),
            ],
            scratch_shapes=[pltpu.VMEM((ROWS, width), BF)],
        ),
        compiler_params=pltpu.CompilerParams(
            dimension_semantics=("arbitrary",), vmem_limit_bytes=LIMIT
        ),
    )(y, patches, gain, wk, wv, wq)


def attention_body(first, last, s_ref, q_ref, kvo_ref, kvs_ref, *refs):
    if first:
        rest = refs
    else:
        acc_in, max_in = refs[:2]
        rest = refs[2:]
    if last:
        o_ref, acc_ref, max_ref = rest
    else:
        acc_ref, max_ref = rest
    if first:
        acc_ref[...] = jnp.zeros(acc_ref.shape, F32)
        max_ref[...] = jnp.full(max_ref.shape, -1e30, F32)
    else:
        acc_ref[...] = acc_in[...]
        max_ref[...] = max_in[...]
    y, x, c, xk, bound0, bound1 = [s_ref[i] for i in range(6)]

    def image_of(row):
        return (row >= bound0).astype(jnp.int32) + (row >= bound1).astype(jnp.int32)

    def block(yy, xx, cc):
        base = ROWS * (8 * yy + 2 * xx + cc)
        return image_of(base), image_of(base + ROWS - 1), 1024 - (base & 1023)

    def row_images(info, dim):
        shape = (ROWS, 1) if dim == 0 else (1, ROWS)
        row = lax.broadcasted_iota(jnp.int32, shape, dim)
        sub = (row >= 96).astype(jnp.int32) + (row >= 192).astype(jnp.int32) + (row >= 288).astype(jnp.int32)
        m = row - 96 * sub
        return jnp.where(m * 4 < info[2], info[0], info[1])

    def update(qb, kb, masks):
        q = q_ref[qb]
        scores, values = [], []
        for n, ref in enumerate((kvo_ref, kvs_ref)):
            s = lax.dot_general(
                q, ref[kb, :, 0:HD], (((1,), (1,)), ((), ())), preferred_element_type=F32
            )
            if masks is not None:
                s = jnp.where(masks[n], s, -1e30)
            scores.append(s)
            values.append(
                jnp.concatenate([ref[kb, :, HD : 2 * HD], jnp.ones((ROWS, HD), BF)], axis=1)
            )
        old = max_ref[qb]
        top = jnp.maximum(
            jnp.max(scores[0], axis=1, keepdims=True), jnp.max(scores[1], axis=1, keepdims=True)
        )
        new = jnp.maximum(old, top)
        factor = jnp.exp(old - new)
        level = new[:, 0:1]
        acc = acc_ref[qb] * jnp.concatenate([factor, factor], axis=1)
        for n in range(2):
            weights = jnp.exp(scores[n] - level)
            if masks is not None:
                weights = jnp.where(masks[n], weights, 0.0)
            acc = acc + cdot(weights.astype(BF), values[n])
        acc_ref[qb] = acc
        max_ref[qb] = new

    def pair(i, carry):
        qb = i >> 2
        kb = i & 3
        qi = block((y - qb) & 3, x, c)
        ki = [block((y - kb) & 3, xk, cc) for cc in (c, 1 - c)]
        low = jnp.minimum(ki[0][0], ki[1][0])
        high = jnp.maximum(ki[0][1], ki[1][1])
        meets = jnp.logical_and(qi[1] >= low, qi[0] <= high)
        uniform = jnp.logical_and(jnp.logical_and(qi[0] == qi[1], low == high), qi[0] == low)

        @pl.when(uniform)
        def _():
            update(qb, kb, None)

        @pl.when(jnp.logical_and(meets, jnp.logical_not(uniform)))
        def _():
            rows = row_images(qi, 0)
            update(qb, kb, [rows == row_images(k, 1) for k in ki])

        return carry

    lax.fori_loop(0, 16, pair, 0)
    if last:
        for b in range(4):
            o_ref[b] = (acc_ref[b, :, 0:HD] / acc_ref[b, :, HD : 2 * HD]).astype(BF)


def attend(scalars, q, kv_own, kv_sib, state, last):
    first = state is None
    state_shapes = [
        jax.ShapeDtypeStruct((4, ROWS, 2 * HD), F32),
        jax.ShapeDtypeStruct((4, ROWS, HD), F32),
    ]
    args = [scalars, q, kv_own, kv_sib] + ([] if first else list(state))

    def body(*refs):
        attention_body(first, last, *refs)

    specs = [SMEM] + [VMEM] * (len(args) - 1)
    if last:
        return call(
            body,
            jax.ShapeDtypeStruct((4, ROWS, HD), BF),
            scratch=[pltpu.VMEM(s.shape, s.dtype) for s in state_shapes],
            in_specs=specs,
        )(*args)
    return call(body, state_shapes, in_specs=specs)(*args)


def out_body(s_ref, o0, o1, o2, o3, w0, w1, w2, w3, x_ref, scale_ref, r_ref, stats_ref):
    y = s_ref[0]
    acc = jnp.zeros((ROWS, w0.shape[1]), F32)
    for o_ref, w_ref in ((o0, w0), (o1, w1), (o2, w2), (o3, w3)):
        heads = jnp.concatenate([o_ref[k] for k in range(4)], axis=1)
        rows = jnp.concatenate(
            [w_ref[pl.ds(pl.multiple_of(HD * ((y + k) & 3), HD), HD), :] for k in range(4)], axis=0
        )
        acc = acc + cdot(heads, rows)
    residual = cdot(sub_row_permutation(), x_ref[...]) + scale_ref[...] * acc
    total = jnp.zeros((MROWS, 1), F32)
    squares = jnp.zeros((MROWS, 1), F32)
    for sub in range(4):
        part = residual[MROWS * sub : MROWS * (sub + 1)]
        r_ref[sub] = part
        total = total + jnp.sum(part, axis=1, keepdims=True)
        squares = squares + jnp.sum(part * part, axis=1, keepdims=True)
    lane = lax.broadcasted_iota(jnp.int32, (MROWS, HD), 1)
    stats_ref[...] = jnp.where(lane == 0, total, squares)


def weight_body(s_ref, own_ref, sib_ref, mine_ref, other_ref):
    c = s_ref[0]
    row = lax.broadcasted_iota(jnp.int32, (128, 128), 0)
    col = lax.broadcasted_iota(jnp.int32, (128, 128), 1)
    perm = jnp.where(4 * (row & 31) + (row >> 5) == col, 1.0, 0.0).astype(BF)
    for b in range(own_ref.shape[0] // 128):
        rows = slice(128 * b, 128 * (b + 1))
        own = cdot(perm, own_ref[rows]).astype(BF)
        sib = cdot(perm, sib_ref[rows]).astype(BF)
        both = jnp.concatenate(
            [jnp.where(c == 0, own, sib), jnp.where(c == 0, sib, own)], axis=1
        )
        dest = slice(32 * b, 32 * (b + 1))
        for i in range(2):
            low = both[32 * i : 32 * (i + 1)]
            high = both[64 + 32 * i : 64 + 32 * (i + 1)]
            mine_ref[i, dest] = jnp.where(c == 0, low, high)
            other_ref[i, dest] = jnp.where(c == 0, high, low)


def projection_body(s_ref, a0, a1, a2, a3, *refs):
    weights = refs[:8]
    out_ref, own_ref, w_ref, sems = refs[8:]
    copies = [pltpu.make_async_copy(weights[n], w_ref.at[n], sems.at[n]) for n in range(8)]
    for copy in copies:
        copy.start()
    y, z, c = s_ref[0], s_ref[1], s_ref[2]
    blocks = []
    for base in (2 * c, 2 - 2 * c):
        for i in range(2):
            blocks.append(jnp.concatenate([a[base + i] for a in (a0, a1, a2, a3)], axis=0))
    for k in range(4):
        copies[2 * k].wait()
        acc = cdot(blocks[0], w_ref[2 * k, 0]) + cdot(blocks[1], w_ref[2 * k, 1])
        copies[2 * k + 1].wait()
        acc = acc + cdot(blocks[2], w_ref[2 * k + 1, 0]) + cdot(blocks[3], w_ref[2 * k + 1, 1])
        target = (y - k - z) & 3
        out_ref[target] = acc.astype(BF)

        @pl.when(target == 0)
        def _(acc=acc):
            own_ref[...] = acc


def place_body(s_ref, r0, r1, r2, r3, slots_ref, text_ref, tslots_ref, own_ref, sib_ref):
    y, x, c = s_ref[0], s_ref[1], s_ref[2]

    def positions(core):
        row = lax.broadcasted_iota(jnp.int32, (448, 1), 0)
        k = (row >= 112).astype(jnp.int32) + (row >= 224).astype(jnp.int32) + (row >= 336).astype(jnp.int32)
        return 112 * (8 * y + 2 * ((x + k) & 3) + core) + row - 112 * k

    def pick(position, slots):
        return jnp.where(position == slots, 1.0, 0.0).astype(BF)

    rows = jnp.concatenate([r[...] for r in (r0, r1, r2, r3)], axis=0)
    mine = positions(c)
    own = cdot(pick(mine, slots_ref[...]), rows) + cdot(pick(mine, tslots_ref[...]), text_ref[...])
    own_ref[...] = own.astype(BF)
    sib_ref[...] = cdot(pick(positions(1 - c), slots_ref[...]), rows).astype(BF)


def stream_body(s_ref, b0, b1, b2, b3, out_ref, squares_ref):
    x = s_ref[0]
    width = b0.shape[1]
    total = jnp.zeros((b0.shape[0], 1), F32)
    blocks = [b0[...], b1[...], b2[...], b3[...]]
    for place in range(4):
        k = (x - place) & 3
        value = blocks[0]
        for n in range(1, 4):
            value = jnp.where(k == n, blocks[n], value)
        out_ref[:, width * place : width * (place + 1)] = value
        wide = value.astype(F32)
        total = total + jnp.sum(wide * wide, axis=1, keepdims=True)
    squares_ref[...] = jnp.broadcast_to(total, squares_ref.shape)


def sum_over_z(value):
    return value + shift(value, "z", 1) + shift(value, "z", 2) + shift(value, "z", 3)


def per_device(
    patches,
    norm_gain,
    query_weight,
    key_weight,
    value_weight,
    out_weight,
    layer_scale,
    merge_gain,
    merge_bias,
    proj_weight,
    proj_bias,
    text_rows,
    stream_gain,
    tile_counts,
    image_slots,
    text_slots,
):
    y, x, c, z = [lax.axis_index(name).astype(jnp.int32) for name in ("y", "x", "c", "z")]
    bounds = jnp.cumsum(tile_counts) * 1024
    width = patches.shape[1]
    share = width // 4

    kv, q = project_qkv(
        y[None], patches, norm_gain[None], key_weight, value_weight, query_weight
    )
    kv_own = jnp.stack([kv[0]] + [shift(kv[k], "y", k) for k in (1, 2, 3)])
    q_own = jnp.stack([q[0]] + [shift(q[k], "y", k) for k in (1, 2, 3)])

    state = None
    for step, k in enumerate((0, 1, 3, 2)):
        kv_now = kv_own if k == 0 else shift(kv_own, "x", k)
        scalars = jnp.stack([y, x, c, (x - k) & 3, bounds[0], bounds[1]])
        state = attend(scalars, q_own, kv_now, swap(kv_now), state, step == 3)
    attended = state
    heads = jnp.stack([attended[0]] + [shift(attended[k], "y", 4 - k) for k in (1, 2, 3)])

    columns = jnp.stack([out_weight[:, share * i : share * (i + 1)] for i in range(4)])
    out_parts = [lax.dynamic_index_in_dim(columns, (z + k) & 3, 0, keepdims=False) for k in range(4)]
    out_parts = [out_parts[0]] + [shift(out_parts[k], "z", k) for k in (1, 2, 3)]
    head_parts = [heads] + [shift(heads, "z", k) for k in (1, 2, 3)]
    patch_columns = jnp.stack([patches[:, share * i : share * (i + 1)] for i in range(4)])
    patch_share = lax.dynamic_index_in_dim(patch_columns, z, 0, keepdims=False)
    scale_share = lax.dynamic_index_in_dim(layer_scale.reshape(4, 1, share), z, 0, keepdims=False)
    residual, stats = call(
        out_body,
        (
            jax.ShapeDtypeStruct((4, MROWS, share), F32),
            jax.ShapeDtypeStruct((MROWS, HD), F32),
        ),
        in_specs=[SMEM] + [VMEM] * 10,
    )(y[None], *head_parts, *out_parts, patch_share, scale_share)
    stats = sum_over_z(stats) * (1.0 / (4 * width))
    mean_row = stats[:, 0:1]
    var_row = stats[:, 1:2] - mean_row * mean_row
    gain = merge_gain.reshape(share, 4).T[:, None, :]
    bias = merge_bias.reshape(share, 4).T[:, None, :]
    merged = ((residual - mean_row) * lax.rsqrt(var_row + 1e-05) * gain + bias).astype(BF)

    mine, other = call(
        weight_body,
        (
            jax.ShapeDtypeStruct((2, share, ROWS), BF),
            jax.ShapeDtypeStruct((2, share, ROWS), BF),
        ),
        in_specs=[SMEM, VMEM, VMEM],
    )(c[None], proj_weight, swap(proj_weight))
    weights = [mine, other]
    for k in (1, 2, 3):
        moved = shift(mine, "y", k)
        weights += [moved, swap(moved)]
    merged_parts = [merged] + [shift(merged, "x", k) for k in (1, 2, 3)]
    partial, own_part = call(
        projection_body,
        (
            jax.ShapeDtypeStruct((4, ROWS, ROWS), BF),
            jax.ShapeDtypeStruct((ROWS, ROWS), F32),
        ),
        scratch=[pltpu.VMEM((8, 2, share, ROWS), BF), pltpu.SemaphoreType.DMA((8,))],
        in_specs=[SMEM] + [VMEM] * 4 + [ANY] * 8,
    )(jnp.stack([y, z, c]), *merged_parts, *weights)
    summed = own_part
    for k in (1, 2, 3):
        summed = summed + shift(partial[k], "z", k).astype(F32)

    turn = [(4 * a + b, 4 * b + a) for a in range(4) for b in range(4)]

    def both_cores(value):
        value = lax.ppermute(value, ("y", "z"), turn)
        sibling = swap(value)
        return jnp.where(
            c == 0,
            jnp.concatenate([value, sibling], axis=1),
            jnp.concatenate([sibling, value], axis=1),
        )

    text = both_cores(text_rows)
    bias_row = both_cores(proj_bias[None])
    rows = jax.nn.gelu(summed + bias_row, approximate=False).astype(BF)

    row_parts = [rows] + [shift(rows, "y", k) for k in (1, 2, 3)]
    order = jnp.arange(4, dtype=jnp.int32)
    slots = image_slots.reshape(4, 4, 2, MROWS)
    slots = lax.dynamic_index_in_dim(slots, c, 2, keepdims=False)
    slots = slots[(y - order) & 3][:, (x - order) & 3].reshape(1, 16 * MROWS)
    placed, for_sibling = call(
        place_body,
        (
            jax.ShapeDtypeStruct((448, ROWS), BF),
            jax.ShapeDtypeStruct((448, ROWS), BF),
        ),
        in_specs=[SMEM] + [VMEM] * 7,
    )(jnp.stack([y, x, c]), *row_parts, slots, text, text_slots[None])
    placed = (placed + swap(for_sibling)).reshape(4, 112, ROWS)
    blocks = [placed[0]] + [shift(placed[k], "x", k) for k in (1, 2, 3)]
    stream, squares = call(
        stream_body,
        (
            jax.ShapeDtypeStruct((112, 4 * ROWS), BF),
            jax.ShapeDtypeStruct((112, HD), F32),
        ),
        in_specs=[SMEM] + [VMEM] * 4,
    )(x[None], *blocks)
    squares = sum_over_z(squares)[:, 0:1]
    inverse_rms = lax.rsqrt(squares * (1.0 / 6144) + 1e-05)
    normed = (stream.astype(F32) * inverse_rms * stream_gain).astype(BF)
    return (stream, normed)


def solution(mesh):
    grid = Mesh(mesh.devices.reshape(4, 4, 2, 4), ("y", "x", "c", "z"))
    seq = ("y", "x", "c")
    return jax.shard_map(
        per_device,
        mesh=grid,
        in_specs=(
            P(seq, None),
            P(),
            P(None, "z"),
            P(None, "z"),
            P(None, "z"),
            P("z", None),
            P(),
            P("z"),
            P("z"),
            P("z", seq),
            P(seq),
            P(None, seq),
            P("z"),
            P(),
            P(),
            P(),
        ),
        out_specs=(P(seq, "z"), P(seq, "z")),
        check_vma=False,
    )
```

time: 982 us -> 356 us (0.36)
  local copies, waits for them, and re-layouts: 279 us -> 39.3 us
  matrix products: 220 us -> 0 us
  waiting for transfers between devices: 333 us -> 132 us
  other arithmetic: 106 us -> 12.8 us
  Pallas kernels: 0 us -> 85.5 us
  starting transfers between devices: 7.72 us -> 81 us
  loops' own time: 16.4 us -> 0 us
  between operations: 14 us -> 1.21 us
    dot_general x53 -> x0, matrix products: 220 us -> none  [the longest x24 102 us: fold_block(): jnp.einsum('hqk,khd->hqd', weights.astype(jnp.bfloat16), value_heads, pre...]
    all_gather x3 -> x0, waiting for transfers between devices: 198 us -> none  [the longest x1 78.9 us: per_device(): lax.all_gather(merged_normed, 'seq', axis=0, tiled=True)]
    dynamic_slice x97 -> x5, local copies, waits for them, and re-layouts: 171 us -> 7.02 us  [the longest x4 7.01 us: per_device(): lax.dynamic_index_in_dim(columns, z + k & 3, 0, keepdims=False)]
    ppermute x0 -> x52, waiting for transfers between devices: none -> 132 us  [the longest x39 129 us: shift(): return lax.ppermute(value, axis, [(i, (i + k) % 4) for i in range(4)])]
    psum x2 -> x0, waiting for transfers between devices: 111 us -> none  [the longest x1 64.3 us: per_device(): lax.psum(branch_part.astype(jnp.bfloat16), 'hid').astype(jnp.float32)]
    reduce_sum x52 -> x0, other arithmetic: 85.7 us -> none  [the longest x24 61.6 us: fold_block(): totals = totals * factor + jnp.sum(weights, axis=-1)]
    pallas_call x0 -> x10, Pallas kernels: none -> 85.5 us  [the longest x3 33.7 us: attend(): return call(body, state_shapes, in_specs=specs)(*args)]
    ppermute x0 -> x52, starting transfers between devices: none -> 81 us  [the longest x39 78.3 us: shift(): return lax.ppermute(value, axis, [(i, (i + k) % 4) for i in range(4)])]
  transfers between devices with their start and end apart: 6 -> 52, of which waited for: 6 -> 29; matrix products, arithmetic and copies ran while one was open for 1% -> 11% of each run, Pallas kernels for 0% -> 20%
where the time goes in v1:
time: 356 us; the launch traced here: 352 us
  waiting for transfers between devices  132 us (37%)
  Pallas kernels  85.5 us (24%)
  starting transfers between devices  81 us (23%)
  local copies, waits for them, and re-layouts  39.3 us (11%)
  other arithmetic  12.8 us (4%)
    ppermute x39, waiting for transfers between devices, shift(): return lax.ppermute(value, axis, [(i, (i + k) % 4) for i in range(4)])  129 us
    ppermute x39, starting transfers between devices, shift(): return lax.ppermute(value, axis, [(i, (i + k) % 4) for i in range(4)])  78.3 us
    pallas_call x3, Pallas kernels, attend(): return call(body, state_shapes, in_specs=specs)(*args)  33.7 us
    pallas_call x1, Pallas kernels, attend(): call(body, jax.ShapeDtypeStruct((4, ROWS, HD), BF), scratch=[pltpu.VMEM(s...  12.3 us
    pallas_call x1, Pallas kernels, per_device(): call(projection_body, (jax.ShapeDtypeStruct((4, ROWS, ROWS), BF), jax.Sha...  12.1 us
    pallas_call x1, Pallas kernels, project_qkv(): pl.pallas_call(qkv_body, out_shape=(jax.ShapeDtypeStruct((4, ROWS, 2 * HD...  11 us
    unnamed x72, local copies, waits for them, and re-layouts  7.87 us
  transfers between devices with their start and end apart: 52, of which 29 were waited for; matrix products, arithmetic and copies ran while one was open for 11% of the time, Pallas kernels for 20%

profile of v1, /device:TPU:0, one launch (start us, length us, event | category | flops | bytes accessed | tf_op | source)
XLA Modules:
  0.0 351.7 jit_solution(15939465999410981254)
XLA Ops:
  2.0 11.0 %shard_map.167 = (bf16[4,384,256]{2,1,0:T(8,128)(2,1)}, bf16[4,384,128]{2,1,0:T(8,128)(2,1)}) custom-call(s32[1]{0:T(128)} %bitcast.1.s_ref, bf16[384,3200]{1,0:T(8,128)(2,1)} %x_ref.1, f32[1,3200]{1,0:T(1,128)} %broadcast_in_dim.9.g_ref, bf16[3200,512]{1,0:T(8,128)(2,1)} %wk_ref.1, bf16[3200,512]{1,0:T(8,128)(2,1)} %wv_ref.1, bf16[3200,512]{1,0:T(8,128)(2,1)} %wq_ref.1), custom_call_target="tpu_custom_call" | custom-call | tf_op jit(solution)/shard_map/pallas_call | solution.py:77
  22.4 5.4 %collective-permute-done.4 = bf16[384,256]{1,0:T(8,128)(2,1)S(1)} collective-permute-done((bf16[384,256]{1,0:T(8,128)(2,1)S(1)}, bf16[384,256]{1,0:T(8,128)(2,1)S(1)}, u32[]{:S(2)}, u32[]{:S(2)}) %collective-permute-start.4) | collective-permute-done | bytes 196640 | tf_op jit(solution)/shard_map/ppermute | solution.py:21
  37.8 11.0 %collective-permute-done.10.refs_2_ = bf16[4,384,256]{2,1,0:T(8,128)(2,1)} collective-permute-done((bf16[4,384,256]{2,1,0:T(8,128)(2,1)S(1)}, bf16[4,384,256]{2,1,0:T(8,128)(2,1)}, u32[]{:S(2)}, u32[]{:S(2)}) %collective-permute-start.10) | collective-permute-done | bytes 786464 | tf_op jit(solution)/shard_map/ppermute | solution.py:21
  48.8 15.0 %collective-permute-done.8.refs_2_ = bf16[4,384,256]{2,1,0:T(8,128)(2,1)} collective-permute-done((bf16[4,384,256]{2,1,0:T(8,128)(2,1)S(1)}, bf16[4,384,256]{2,1,0:T(8,128)(2,1)}, u32[]{:S(2)}, u32[]{:S(2)}) %collective-permute-start.8) | collective-permute-done | bytes 786464 | tf_op jit(solution)/shard_map/ppermute | solution.py:21
  90.6 10.1 %shard_map.168 = (f32[4,384,256]{2,1,0:T(8,128)}, f32[4,384,128]{2,1,0:T(8,128)}) custom-call(s32[6]{0:T(128)} %stack.140.refs_0_, bf16[4,384,128]{2,1,0:T(8,128)(2,1)} %pad_maximum_fusion.2.refs_1_, bf16[4,384,256]{2,1,0:T(8,128)(2,1)} %copy-done.2, bf16[4,384,256]{2,1,0:T(8,128)(2,1)} %collective-permute-done.12.refs_3_), custom_call_target="tpu_custom_call" | custom-call | tf_op jit(solution)/shard_map/pallas_call | solution.py:206
  104.2 11.9 %shard_map.169 = (f32[4,384,256]{2,1,0:T(8,128)}, f32[4,384,128]{2,1,0:T(8,128)}) custom-call(s32[6]{0:T(128)} %stack.138.refs_0_, bf16[4,384,128]{2,1,0:T(8,128)(2,1)} %pad_maximum_fusion.2.refs_1_, bf16[4,384,256]{2,1,0:T(8,128)(2,1)} %collective-permute-done.10.refs_2_, bf16[4,384,256]{2,1,0:T(8,128)(2,1)} %collective-permute-done.11.refs_3_, ...), custom_call_target="tpu_custom_call" | custom-call | tf_op jit(solution)/shard_map/pallas_call | solution.py:206
  117.1 11.8 %shard_map.170 = (f32[4,384,256]{2,1,0:T(8,128)}, f32[4,384,128]{2,1,0:T(8,128)}) custom-call(s32[6]{0:T(128)} %stack.136.refs_0_, bf16[4,384,128]{2,1,0:T(8,128)(2,1)} %pad_maximum_fusion.2.refs_1_, bf16[4,384,256]{2,1,0:T(8,128)(2,1)} %collective-permute-done.8.refs_2_, bf16[4,384,256]{2,1,0:T(8,128)(2,1)} %collective-permute-done.9.refs_3_, ...), custom_call_target="tpu_custom_call" | custom-call | tf_op jit(solution)/shard_map/pallas_call | solution.py:206
  128.9 12.3 %shard_map.171 = bf16[4,384,128]{2,1,0:T(8,128)(2,1)} custom-call(s32[6]{0:T(128)} %stack.126.refs_0_, bf16[4,384,128]{2,1,0:T(8,128)(2,1)} %pad_maximum_fusion.2.refs_1_, bf16[4,384,256]{2,1,0:T(8,128)(2,1)} %collective-permute-done.6.refs_2_, bf16[4,384,256]{2,1,0:T(8,128)(2,1)} %collective-permute-done.7.refs_3_, ...), custom_call_target="tpu_custom_call" | custom-call | tf_op jit(solution)/shard_map/pallas_call | solution.py:200
  148.4 4.7 %collective-permute-done.14 = bf16[384,128]{1,0:T(8,128)(2,1)S(1)} collective-permute-done((bf16[384,128]{1,0:T(8,128)(2,1)S(1)}, bf16[384,128]{1,0:T(8,128)(2,1)S(1)}, u32[]{:S(2)}, u32[]{:S(2)}) %collective-permute-start.14) | collective-permute-done | bytes 98336 | tf_op jit(solution)/shard_map/ppermute | solution.py:21
  153.6 5.3 %collective-permute-done.15 = bf16[384,128]{1,0:T(8,128)(2,1)S(1)} collective-permute-done((bf16[384,128]{1,0:T(8,128)(2,1)S(1)}, bf16[384,128]{1,0:T(8,128)(2,1)S(1)}, u32[]{:S(2)}, u32[]{:S(2)}) %collective-permute-start.15) | collective-permute-done | bytes 98336 | tf_op jit(solution)/shard_map/ppermute | solution.py:21
  165.4 4.6 %shard_map.173 = (bf16[2,800,384]{2,1,0:T(8,128)(2,1)}, bf16[2,800,384]{2,1,0:T(8,128)(2,1)}) custom-call(s32[1]{0:T(128)} %bitcast.2.s_ref, bf16[3200,192]{1,0:T(8,128)(2,1)} %copy.49.own_ref, bf16[3200,192]{1,0:T(8,128)(2,1)} %copy.50.sib_ref), custom_call_target="tpu_custom_call" | custom-call | tf_op jit(solution)/shard_map/pallas_call | solution.py:371
  186.6 4.1 %collective-permute-done.18.o3 = bf16[4,384,128]{2,1,0:T(8,128)(2,1)} collective-permute-done((bf16[4,384,128]{2,1,0:T(8,128)(2,1)S(1)}, bf16[4,384,128]{2,1,0:T(8,128)(2,1)}, u32[]{:S(2)}, u32[]{:S(2)}) %collective-permute-start.18) | collective-permute-done | bytes 393248 | tf_op jit(solution)/shard_map/ppermute | solution.py:21
  190.7 6.0 %shard_map.172 = (f32[4,96,800]{2,1,0:T(8,128)}, f32[96,128]{1,0:T(8,128)}) custom-call(s32[1]{0:T(128)} %bitcast.1.s_ref, bf16[4,384,128]{2,1,0:T(8,128)(2,1)} %copy-done.4, bf16[4,384,128]{2,1,0:T(8,128)(2,1)} %copy-done.11, bf16[4,384,128]{2,1,0:T(8,128)(2,1)} %collective-permute-done.17.o2, bf16[4,384,128]{2,1,0:T(8,128)(2,1)} %collective-permute-done.18.o3, ...), custom_call_target="tpu_custom_call" | custom-call | tf_op jit(solution)/shard_map/pallas_call | solution.py:356
  207.1 5.5 %collective-permute-start.25 = (bf16[4,96,800]{2,1,0:T(8,128)(2,1)S(1)}, bf16[4,96,800]{2,1,0:T(8,128)(2,1)S(1)}, u32[]{:S(2)}, u32[]{:S(2)}) collective-permute-start(bf16[4,96,800]{2,1,0:T(8,128)(2,1)S(1)} %add_convert_fusion.a0), channel_id=1, source_target_pairs={{0,8},{8,16},{16,24},{24,0},{1,9},{9,17},{17,25},{25,1},{2,10},{10... | collective-permute-start | bytes 1843208 | tf_op jit(solution)/shard_map/ppermute | solution.py:21
  212.7 10.3 %collective-permute-done.31.refs_4_ = bf16[2,800,384]{2,1,0:T(8,128)(2,1)} collective-permute-done((bf16[2,800,384]{2,1,0:T(8,128)(2,1)}, bf16[2,800,384]{2,1,0:T(8,128)(2,1)}, u32[]{:S(2)}, u32[]{:S(2)}) %collective-permute-start.31) | collective-permute-done | bytes 1228832 | tf_op jit(solution)/shard_map/ppermute | solution.py:21
  223.9 10.2 %collective-permute-start.26 = (bf16[4,96,800]{2,1,0:T(8,128)(2,1)S(1)}, bf16[4,96,800]{2,1,0:T(8,128)(2,1)}, u32[]{:S(2)}, u32[]{:S(2)}) collective-permute-start(bf16[4,96,800]{2,1,0:T(8,128)(2,1)S(1)} %add_convert_fusion.a0), channel_id=1, source_target_pairs={{0,16},{8,24},{16,0},{24,8},{1,17},{9,25},{17,1},{25,9},{2,18},{10... | collective-permute-start | bytes 1843208 | tf_op jit(solution)/shard_map/ppermute | solution.py:21
  236.9 13.0 %collective-permute-done.26.a2 = bf16[4,96,800]{2,1,0:T(8,128)(2,1)} collective-permute-done((bf16[4,96,800]{2,1,0:T(8,128)(2,1)S(1)}, bf16[4,96,800]{2,1,0:T(8,128)(2,1)}, u32[]{:S(2)}, u32[]{:S(2)}) %collective-permute-start.26) | collective-permute-done | bytes 614432 | tf_op jit(solution)/shard_map/ppermute | solution.py:21
  250.6 15.5 %collective-permute-done.27.a3 = bf16[4,96,800]{2,1,0:T(8,128)(2,1)} collective-permute-done((bf16[4,96,800]{2,1,0:T(8,128)(2,1)S(1)}, bf16[4,96,800]{2,1,0:T(8,128)(2,1)}, u32[]{:S(2)}, u32[]{:S(2)}) %collective-permute-start.27) | collective-permute-done | bytes 614432 | tf_op jit(solution)/shard_map/ppermute | solution.py:21
  269.1 12.1 %shard_map.174 = (bf16[4,384,384]{2,1,0:T(8,128)(2,1)}, f32[384,384]{1,0:T(8,128)}) custom-call(s32[3]{0:T(128)} %add_add_fusion.2.s_ref, bf16[4,96,800]{2,1,0:T(8,128)(2,1)} %copy-done.3, bf16[4,96,800]{2,1,0:T(8,128)(2,1)} %copy-done.9, bf16[4,96,800]{2,1,0:T(8,128)(2,1)} %collective-permute-done.26.a2, bf16[4,96,800]{2,1,0:T(8,128)(2,1)} %collective-permute-done.27.a3, ...), custom_call_target="tpu_custom_call" | custom-call | tf_op jit(solution)/shard_map/pallas_call | solution.py:384
  284.8 4.8 %collective-permute-start.36 = (bf16[384,384]{1,0:T(8,128)(2,1)S(1)}, bf16[384,384]{1,0:T(8,128)(2,1)S(1)}, u32[]{:S(2)}, u32[]{:S(2)}) collective-permute-start(bf16[384,384]{1,0:T(8,128)(2,1)S(1)} %get-tuple-element.54), channel_id=1, source_target_pairs={{0,2},{1,3},{2,0},{3,1},{4,6},{5,7},{6,4},{7,5},{8,10},{9,11},{10,... | collective-permute-start | bytes 884744 | tf_op jit(solution)/shard_map/ppermute | solution.py:21
  291.1 4.0 %collective-permute-done.35 = bf16[384,384]{1,0:T(8,128)(2,1)S(1)} collective-permute-done((bf16[384,384]{1,0:T(8,128)(2,1)S(1)}, bf16[384,384]{1,0:T(8,128)(2,1)S(1)}, u32[]{:S(2)}, u32[]{:S(2)}) %collective-permute-start.35) | collective-permute-done | bytes 294944 | tf_op jit(solution)/shard_map/ppermute | solution.py:21
  295.1 7.1 %collective-permute-done.36 = bf16[384,384]{1,0:T(8,128)(2,1)S(1)} collective-permute-done((bf16[384,384]{1,0:T(8,128)(2,1)S(1)}, bf16[384,384]{1,0:T(8,128)(2,1)S(1)}, u32[]{:S(2)}, u32[]{:S(2)}) %collective-permute-start.36) | collective-permute-done | bytes 294944 | tf_op jit(solution)/shard_map/ppermute | solution.py:21
  313.9 5.4 %collective-permute-done.41.r2 = bf16[384,384]{1,0:T(8,128)(2,1)S(1)} collective-permute-done((bf16[384,384]{1,0:T(8,128)(2,1)S(1)}, bf16[384,384]{1,0:T(8,128)(2,1)S(1)}, u32[]{:S(2)}, u32[]{:S(2)}) %collective-permute-start.41) | collective-permute-done | bytes 294944 | tf_op jit(solution)/shard_map/ppermute | solution.py:21
  320.2 3.9 %shard_map.175 = (bf16[448,384]{1,0:T(8,128)(2,1)}, bf16[448,384]{1,0:T(8,128)(2,1)}) custom-call(s32[3]{0:T(128)} %add_add_fusion.1.s_ref, bf16[384,384]{1,0:T(8,128)(2,1)} %copy-done.8, bf16[384,384]{1,0:T(8,128)(2,1)} %copy-done.14, bf16[384,384]{1,0:T(8,128)(2,1)} %copy-done.15, bf16[384,384]{1,0:T(8,128)(2,1)} %copy-done.16, ...), custom_call_target="tpu_custom_call" | custom-call | tf_op jit(solution)/shard_map/pallas_call | solution.py:417
  (217 shorter events, 145.4 us)
Async XLA Ops:
  27.9 20.9 %collective-permute-start.10 = (bf16[4,384,256]{2,1,0:T(8,128)(2,1)S(1)}, bf16[4,384,256]{2,1,0:T(8,128)(2,1)}, u32[]{:S(2)}, u32[]{:S(2)}) collective-permute-start(bf16[4,384,256]{2,1,0:T(8,128)(2,1)S(1)} %pad_maximum_fusion.1.refs_2_), channel_id=1, source_target_pairs={{0,8},{8,16},{16,24},{24,0},{1,9},{9,17},{17,25},{25,1},{2,10},{10... | collective-permute-start | bytes 2359304 | tf_op jit(solution)/shard_map/ppermute | solution.py:21
  29.5 34.3 %collective-permute-start.8 = (bf16[4,384,256]{2,1,0:T(8,128)(2,1)S(1)}, bf16[4,384,256]{2,1,0:T(8,128)(2,1)}, u32[]{:S(2)}, u32[]{:S(2)}) collective-permute-start(bf16[4,384,256]{2,1,0:T(8,128)(2,1)S(1)} %pad_maximum_fusion.1.refs_2_), channel_id=1, source_target_pairs={{0,24},{8,0},{16,8},{24,16},{1,25},{9,1},{17,9},{25,17},{2,26},{10... | collective-permute-start | bytes 2359304 | tf_op jit(solution)/shard_map/ppermute | solution.py:21
  31.2 34.3 %collective-permute-start.6 = (bf16[4,384,256]{2,1,0:T(8,128)(2,1)S(1)}, bf16[4,384,256]{2,1,0:T(8,128)(2,1)}, u32[]{:S(2)}, u32[]{:S(2)}) collective-permute-start(bf16[4,384,256]{2,1,0:T(8,128)(2,1)S(1)} %pad_maximum_fusion.1.refs_2_), channel_id=1, source_target_pairs={{0,16},{8,24},{16,0},{24,8},{1,17},{9,25},{17,1},{25,9},{2,18},{10... | collective-permute-start | bytes 2359304 | tf_op jit(solution)/shard_map/ppermute | solution.py:21
  33.7 34.1 %collective-permute-start.1 = (bf16[384,128]{1,0:T(8,128)(2,1)S(1)}, bf16[384,128]{1,0:T(8,128)(2,1)S(1)}, u32[]{:S(2)}, u32[]{:S(2)}) collective-permute-start(bf16[384,128]{1,0:T(8,128)(2,1)S(1)} %get-tuple-element.65), channel_id=1, source_target_pairs={{0,64},{32,96},{64,0},{96,32},{1,65},{33,97},{65,1},{97,33},{2,66}... | collective-permute-start | bytes 294920 | tf_op jit(solution)/shard_map/ppermute | solution.py:21
  37.8 50.7 %collective-permute-start.12 = (bf16[4,384,256]{2,1,0:T(8,128)(2,1)S(1)}, bf16[4,384,256]{2,1,0:T(8,128)(2,1)}, u32[]{:S(2)}, u32[]{:S(2)}) collective-permute-start(bf16[4,384,256]{2,1,0:T(8,128)(2,1)S(1)} %pad_maximum_fusion.1.refs_2_), channel_id=1, source_target_pairs={{0,4},{4,0},{1,5},{5,1},{2,6},{6,2},{3,7},{7,3},{8,12},{12,8},{9,1... | collective-permute-start | bytes 2359304 | tf_op jit(solution)/shard_map/ppermute | solution.py:25
  48.8 51.8 %collective-permute-start.11 = (bf16[4,384,256]{2,1,0:T(8,128)(2,1)}, bf16[4,384,256]{2,1,0:T(8,128)(2,1)}, u32[]{:S(2)}, u32[]{:S(2)}) collective-permute-start(bf16[4,384,256]{2,1,0:T(8,128)(2,1)} %collective-permute-done.10.refs_2_), channel_id=1, source_target_pairs={{0,4},{4,0},{1,5},{5,1},{2,6},{6,2},{3,7},{7,3},{8,12},{12,8},{9,1... | collective-permute-start | bytes 2359304 | tf_op jit(solution)/shard_map/ppermute | solution.py:25
  63.8 52.3 %collective-permute-start.9 = (bf16[4,384,256]{2,1,0:T(8,128)(2,1)}, bf16[4,384,256]{2,1,0:T(8,128)(2,1)}, u32[]{:S(2)}, u32[]{:S(2)}) collective-permute-start(bf16[4,384,256]{2,1,0:T(8,128)(2,1)} %collective-permute-done.8.refs_2_), channel_id=1, source_target_pairs={{0,4},{4,0},{1,5},{5,1},{2,6},{6,2},{3,7},{7,3},{8,12},{12,8},{9,1... | collective-permute-start | bytes 2359304 | tf_op jit(solution)/shard_map/ppermute | solution.py:25
  65.6 63.3 %collective-permute-start.7 = (bf16[4,384,256]{2,1,0:T(8,128)(2,1)}, bf16[4,384,256]{2,1,0:T(8,128)(2,1)}, u32[]{:S(2)}, u32[]{:S(2)}) collective-permute-start(bf16[4,384,256]{2,1,0:T(8,128)(2,1)} %collective-permute-done.6.refs_2_), channel_id=1, source_target_pairs={{0,4},{4,0},{1,5},{5,1},{2,6},{6,2},{3,7},{7,3},{8,12},{12,8},{9,1... | collective-permute-start | bytes 2359304 | tf_op jit(solution)/shard_map/ppermute | solution.py:25
  80.6 82.2 %collective-permute-start.28 = (bf16[3200,192]{0,1:T(8,128)(2,1)}, bf16[3200,192]{0,1:T(8,128)(2,1)}, u32[]{:S(2)}, u32[]{:S(2)}) collective-permute-start(bf16[3200,192]{0,1:T(8,128)(2,1)} %param.25), channel_id=1, source_target_pairs={{0,4},{4,0},{1,5},{5,1},{2,6},{6,2},{3,7},{7,3},{8,12},{12,8},{9,1... | collective-permute-start | bytes 3686408 | tf_op jit(solution)/shard_map/ppermute | solution.py:25
  88.5 81.5 %collective-permute-start.19 = (bf16[512,800]{0,1:T(8,128)(2,1)}, bf16[512,800]{0,1:T(8,128)(2,1)}, u32[]{:S(2)}, u32[]{:S(2)}) collective-permute-start(bf16[512,800]{0,1:T(8,128)(2,1)} %bitcast.33), channel_id=1, source_target_pairs={{0,1},{1,2},{2,3},{3,0},{4,5},{5,6},{6,7},{7,4},{8,9},{9,10},{10,1... | collective-permute-start | bytes 2457608 | tf_op jit(solution)/shard_map/ppermute | solution.py:21
  100.6 73.2 %collective-permute-start.20 = (bf16[512,800]{0,1:T(8,128)(2,1)}, bf16[512,800]{0,1:T(8,128)(2,1)}, u32[]{:S(2)}, u32[]{:S(2)}) collective-permute-start(bf16[512,800]{0,1:T(8,128)(2,1)} %bitcast.34), channel_id=1, source_target_pairs={{0,2},{1,3},{2,0},{3,1},{4,6},{5,7},{6,4},{7,5},{8,10},{9,11},{10,... | collective-permute-start | bytes 2457608 | tf_op jit(solution)/shard_map/ppermute | solution.py:21
  116.1 58.5 %collective-permute-start.21 = (bf16[512,800]{0,1:T(8,128)(2,1)}, bf16[512,800]{0,1:T(8,128)(2,1)}, u32[]{:S(2)}, u32[]{:S(2)}) collective-permute-start(bf16[512,800]{0,1:T(8,128)(2,1)} %bitcast.35), channel_id=1, source_target_pairs={{0,3},{1,0},{2,1},{3,2},{4,7},{5,4},{6,5},{7,6},{8,11},{9,8},{10,9... | collective-permute-start | bytes 2457608 | tf_op jit(solution)/shard_map/ppermute | solution.py:21
  170.0 42.6 %collective-permute-start.29 = (bf16[2,800,384]{2,1,0:T(8,128)(2,1)}, bf16[2,800,384]{2,1,0:T(8,128)(2,1)}, u32[]{:S(2)}, u32[]{:S(2)}) collective-permute-start(bf16[2,800,384]{2,1,0:T(8,128)(2,1)} %get-tuple-element.30.refs_0_), channel_id=1, source_target_pairs={{0,32},{32,64},{64,96},{96,0},{1,33},{33,65},{65,97},{97,1},{2,34}... | collective-permute-start | bytes 3686408 | tf_op jit(solution)/shard_map/ppermute | solution.py:21
  170.0 52.9 %collective-permute-start.31 = (bf16[2,800,384]{2,1,0:T(8,128)(2,1)}, bf16[2,800,384]{2,1,0:T(8,128)(2,1)}, u32[]{:S(2)}, u32[]{:S(2)}) collective-permute-start(bf16[2,800,384]{2,1,0:T(8,128)(2,1)} %get-tuple-element.30.refs_0_), channel_id=1, source_target_pairs={{0,64},{32,96},{64,0},{96,32},{1,65},{33,97},{65,1},{97,33},{2,66}... | collective-permute-start | bytes 3686408 | tf_op jit(solution)/shard_map/ppermute | solution.py:21
  173.8 50.1 %collective-permute-start.33 = (bf16[2,800,384]{2,1,0:T(8,128)(2,1)}, bf16[2,800,384]{2,1,0:T(8,128)(2,1)}, u32[]{:S(2)}, u32[]{:S(2)}) collective-permute-start(bf16[2,800,384]{2,1,0:T(8,128)(2,1)} %get-tuple-element.30.refs_0_), channel_id=1, source_target_pairs={{0,96},{32,0},{64,32},{96,64},{1,97},{33,1},{65,33},{97,65},{2,98}... | collective-permute-start | bytes 3686408 | tf_op jit(solution)/shard_map/ppermute | solution.py:21
  207.1 27.1 %collective-permute-start.25 = (bf16[4,96,800]{2,1,0:T(8,128)(2,1)S(1)}, bf16[4,96,800]{2,1,0:T(8,128)(2,1)S(1)}, u32[]{:S(2)}, u32[]{:S(2)}) collective-permute-start(bf16[4,96,800]{2,1,0:T(8,128)(2,1)S(1)} %add_convert_fusion.a0), channel_id=1, source_target_pairs={{0,8},{8,16},{16,24},{24,0},{1,9},{9,17},{17,25},{25,1},{2,10},{10... | collective-permute-start | bytes 1843208 | tf_op jit(solution)/shard_map/ppermute | solution.py:21
  212.7 55.0 %collective-permute-start.30 = (bf16[2,800,384]{2,1,0:T(8,128)(2,1)}, bf16[2,800,384]{2,1,0:T(8,128)(2,1)S(1)}, u32[]{:S(2)}, u32[]{:S(2)}) collective-permute-start(bf16[2,800,384]{2,1,0:T(8,128)(2,1)} %collective-permute-done.29.refs_2_), channel_id=1, source_target_pairs={{0,4},{4,0},{1,5},{5,1},{2,6},{6,2},{3,7},{7,3},{8,12},{12,8},{9,1... | collective-permute-start | bytes 3686408 | tf_op jit(solution)/shard_map/ppermute | solution.py:25
  222.9 44.7 %collective-permute-start.32 = (bf16[2,800,384]{2,1,0:T(8,128)(2,1)}, bf16[2,800,384]{2,1,0:T(8,128)(2,1)S(1)}, u32[]{:S(2)}, u32[]{:S(2)}) collective-permute-start(bf16[2,800,384]{2,1,0:T(8,128)(2,1)} %collective-permute-done.31.refs_4_), channel_id=1, source_target_pairs={{0,4},{4,0},{1,5},{5,1},{2,6},{6,2},{3,7},{7,3},{8,12},{12,8},{9,1... | collective-permute-start | bytes 3686408 | tf_op jit(solution)/shard_map/ppermute | solution.py:25
  223.9 43.7 %collective-permute-start.34 = (bf16[2,800,384]{2,1,0:T(8,128)(2,1)}, bf16[2,800,384]{2,1,0:T(8,128)(2,1)}, u32[]{:S(2)}, u32[]{:S(2)}) collective-permute-start(bf16[2,800,384]{2,1,0:T(8,128)(2,1)} %collective-permute-done.33.refs_6_), channel_id=1, source_target_pairs={{0,4},{4,0},{1,5},{5,1},{2,6},{6,2},{3,7},{7,3},{8,12},{12,8},{9,1... | collective-permute-start | bytes 3686408 | tf_op jit(solution)/shard_map/ppermute | solution.py:25
  223.9 25.9 %collective-permute-start.26 = (bf16[4,96,800]{2,1,0:T(8,128)(2,1)S(1)}, bf16[4,96,800]{2,1,0:T(8,128)(2,1)}, u32[]{:S(2)}, u32[]{:S(2)}) collective-permute-start(bf16[4,96,800]{2,1,0:T(8,128)(2,1)S(1)} %add_convert_fusion.a0), channel_id=1, source_target_pairs={{0,16},{8,24},{16,0},{24,8},{1,17},{9,25},{17,1},{25,9},{2,18},{10... | collective-permute-start | bytes 1843208 | tf_op jit(solution)/shard_map/ppermute | solution.py:21
  235.0 31.0 %collective-permute-start.27 = (bf16[4,96,800]{2,1,0:T(8,128)(2,1)S(1)}, bf16[4,96,800]{2,1,0:T(8,128)(2,1)}, u32[]{:S(2)}, u32[]{:S(2)}) collective-permute-start(bf16[4,96,800]{2,1,0:T(8,128)(2,1)S(1)} %add_convert_fusion.a0), channel_id=1, source_target_pairs={{0,24},{8,0},{16,8},{24,16},{1,25},{9,1},{17,9},{25,17},{2,26},{10... | collective-permute-start | bytes 1843208 | tf_op jit(solution)/shard_map/ppermute | solution.py:21
  249.9 39.7 %collective-permute-start.38 = (f32[1,192]{1,0:T(1,128)S(1)}, f32[1,192]{1,0:T(1,128)S(1)}, u32[]{:S(2)}, u32[]{:S(2)}) collective-permute-start(f32[1,192]{1,0:T(1,128)S(1)} %bitcast.97), channel_id=1, source_target_pairs={{0,0},{1,32},{2,64},{3,96},{32,1},{33,33},{34,65},{35,97},{64,2},{... | collective-permute-start | bytes 2312 | tf_op jit(solution)/shard_map/ppermute | solution.py:400
  266.1 24.8 %collective-permute-start.43 = (bf16[512,192]{1,0:T(8,128)(2,1)}, bf16[512,192]{1,0:T(8,128)(2,1)S(1)}, u32[]{:S(2)}, u32[]{:S(2)}) collective-permute-start(bf16[512,192]{1,0:T(8,128)(2,1)} %copy.53), channel_id=1, source_target_pairs={{0,0},{1,32},{2,64},{3,96},{32,1},{33,33},{34,65},{35,97},{64,2},{... | collective-permute-start | bytes 589832 | tf_op jit(solution)/shard_map/ppermute | solution.py:400
  290.9 18.5 %collective-permute-start.44 = (bf16[512,192]{1,0:T(8,128)(2,1)S(1)}, bf16[512,192]{1,0:T(8,128)(2,1)S(1)}, u32[]{:S(2)}, u32[]{:S(2)}) collective-permute-start(bf16[512,192]{1,0:T(8,128)(2,1)S(1)} %collective-permute-done.43), channel_id=1, source_target_pairs={{0,4},{4,0},{1,5},{5,1},{2,6},{6,2},{3,7},{7,3},{8,12},{12,8},{9,1... | collective-permute-start | bytes 589832 | tf_op jit(solution)/shard_map/ppermute | solution.py:25
  (63 other events, 647.2 us)

commit v2 on v1

v2 whole, which is shorter than its diff:
```python
import jax
import jax.numpy as jnp
from jax import lax
from jax.experimental import pallas as pl
from jax.experimental.pallas import tpu as pltpu
from jax.sharding import Mesh, PartitionSpec as P

HD = 128
ROWS = 384
MROWS = 96
BF = jnp.bfloat16
F32 = jnp.float32
LIMIT = 60 * 1024 * 1024


def cdot(a, b):
    return jnp.dot(a, b, preferred_element_type=F32)


def shift(value, axis, k):
    return lax.ppermute(value, axis, [(i, (i + k) % 4) for i in range(4)])


def swap(value):
    return lax.ppermute(value, "c", [(0, 1), (1, 0)])


def cost(us):
    return pl.CostEstimate(flops=int(us * 1.0e9), transcendentals=0, bytes_accessed=0)


def call(body, out_shape, us, scratch=(), **kw):
    return pl.pallas_call(
        body,
        out_shape=out_shape,
        scratch_shapes=scratch,
        cost_estimate=cost(us),
        compiler_params=pltpu.CompilerParams(vmem_limit_bytes=LIMIT),
        **kw,
    )


SMEM = pl.BlockSpec(memory_space=pltpu.SMEM)
VMEM = pl.BlockSpec(memory_space=pltpu.VMEM)
ANY = pl.BlockSpec(memory_space=pl.ANY)


def sub_row_permutation():
    row = lax.broadcasted_iota(jnp.int32, (ROWS, ROWS), 0)
    col = lax.broadcasted_iota(jnp.int32, (ROWS, ROWS), 1)
    sub = (row >= 96).astype(jnp.int32) + (row >= 192).astype(jnp.int32) + (row >= 288).astype(jnp.int32)
    m = row - 96 * sub
    source = (2 * (m >> 4) + (sub >> 1)) * 32 + 2 * (m & 15) + (sub & 1)
    return jnp.where(source == col, 1.0, 0.0).astype(BF)


def qkv_body(s_ref, x_ref, g_ref, wk_ref, wv_ref, wq_ref, kvq_ref, xn_ref):
    half = pl.program_id(0)

    @pl.when(half == 0)
    def _():
        xf = cdot(sub_row_permutation(), x_ref[...])
        scale = lax.rsqrt(jnp.mean(xf * xf, axis=-1, keepdims=True) + 1e-06)
        xn_ref[...] = (xf * scale * g_ref[...]).astype(BF)

    xn = xn_ref[...]
    keys = cdot(xn, wk_ref[...]).astype(BF)
    values = cdot(xn, wv_ref[...]).astype(BF)
    queries = (cdot(xn, wq_ref[...]) * HD ** (-0.5)).astype(BF)
    for i in range(2):
        slot = (2 * half + i - s_ref[0]) & 3
        part = slice(HD * i, HD * (i + 1))
        kvq_ref[slot, :, 0:HD] = keys[:, part]
        kvq_ref[slot, :, HD : 2 * HD] = values[:, part]
        kvq_ref[slot, :, 2 * HD : 3 * HD] = queries[:, part]


def project_qkv(y, patches, gain, wk, wv, wq):
    width = patches.shape[1]
    whole = pl.BlockSpec((ROWS, width), lambda j, s: (0, 0))
    weight = pl.BlockSpec((width, 2 * HD), lambda j, s: (0, j))
    return pl.pallas_call(
        qkv_body,
        out_shape=jax.ShapeDtypeStruct((4, ROWS, 3 * HD), BF),
        grid_spec=pltpu.PrefetchScalarGridSpec(
            num_scalar_prefetch=1,
            grid=(2,),
            in_specs=[whole, pl.BlockSpec((1, width), lambda j, s: (0, 0)), weight, weight, weight],
            out_specs=pl.BlockSpec((4, ROWS, 3 * HD), lambda j, s: (0, 0, 0)),
            scratch_shapes=[pltpu.VMEM((ROWS, width), BF)],
        ),
        cost_estimate=cost(11),
        compiler_params=pltpu.CompilerParams(
            dimension_semantics=("arbitrary",), vmem_limit_bytes=LIMIT
        ),
    )(y, patches, gain, wk, wv, wq)


def image_lanes(info, scale, same):
    row = lax.broadcasted_iota(jnp.int32, (ROWS, HD), 0)
    lane = lax.broadcasted_iota(jnp.int32, (ROWS, HD), 1)
    sub = (row >= 96).astype(jnp.int32) + (row >= 192).astype(jnp.int32) + (row >= 288).astype(jnp.int32)
    image = jnp.where((row - 96 * sub) * 4 < info[2], info[0], info[1])
    hit = lane == image if same else lane != image
    return jnp.where(hit, scale, 0.0).astype(BF)


def attention_body(steps, first, last, s_ref, t_ref, q_ref, *refs):
    rest = refs[:-2]
    own_ref, sib_ref = refs[-2:]
    filled = 0
    while filled < len(steps):
        own, sib = rest[:2]
        rest = rest[2:]
        own_ref[filled : filled + own.shape[0]] = own[...]
        sib_ref[filled : filled + own.shape[0]] = sib[...]
        filled += own.shape[0]
    if not first:
        acc_in, max_in = rest[:2]
        rest = rest[2:]
    if last:
        o_ref, acc_ref, max_ref = rest
    else:
        acc_ref, max_ref = rest
    if first:
        acc_ref[...] = jnp.zeros(acc_ref.shape, F32)
        max_ref[...] = jnp.full(max_ref.shape, -1e30, F32)
    else:
        acc_ref[...] = acc_in[...]
        max_ref[...] = max_in[...]
    y, x, c = s_ref[0], s_ref[1], s_ref[2]
    bound0 = 1024 * t_ref[0]
    bound1 = 1024 * (t_ref[0] + t_ref[1])

    def image_of(row):
        return (row >= bound0).astype(jnp.int32) + (row >= bound1).astype(jnp.int32)

    def block(yy, xx, cc):
        base = ROWS * (8 * yy + 2 * xx + cc)
        return image_of(base), image_of(base + ROWS - 1), 1024 - (base & 1023)

    def update(qb, kr, qi, ki):
        marks = image_lanes(qi, -1e30, False)
        keys, values = [], []
        for n, ref in enumerate((own_ref, sib_ref)):
            keys.append(jnp.concatenate([ref[kr, :, 0:HD], image_lanes(ki[n], 1.0, True)], axis=1))
            values.append(
                jnp.concatenate([ref[kr, :, HD : 2 * HD], jnp.ones((ROWS, HD), BF)], axis=1)
            )
        keys = jnp.concatenate(keys, axis=0)
        values = jnp.concatenate(values, axis=0)
        half = ROWS // 2

        def score(rows):
            q = jnp.concatenate([q_ref[qb, rows, :], marks[rows]], axis=1)
            return lax.dot_general(q, keys, (((1,), (1,)), ((), ())), preferred_element_type=F32)

        def fold(rows, scores):
            old = max_ref[qb, rows]
            new = jnp.maximum(old, jnp.max(scores, axis=1, keepdims=True))
            factor = jnp.exp(old - new)
            weights = jnp.exp(scores - new[:, 0:1]).astype(BF)
            acc = acc_ref[qb, rows] * jnp.concatenate([factor, factor], axis=1)
            acc_ref[qb, rows] = acc + cdot(weights, values)
            max_ref[qb, rows] = new

        upper, lower = slice(0, half), slice(half, ROWS)
        first_scores = score(upper)
        second_scores = score(lower)
        fold(upper, first_scores)
        fold(lower, second_scores)

    def pair(i, carry):
        qb = i & 3
        kr = i >> 2
        qi = block((y - qb) & 3, x, c)
        step = steps[0] if len(steps) == 4 else jnp.where(kr < 4, steps[0], steps[4])
        xk = (x - step) & 3
        ki = [block((y - kr) & 3, xk, cc) for cc in (c, 1 - c)]
        low = jnp.minimum(ki[0][0], ki[1][0])
        high = jnp.maximum(ki[0][1], ki[1][1])

        @pl.when(jnp.logical_and(qi[1] >= low, qi[0] <= high))
        def _():
            update(qb, kr, qi, ki)

        return carry

    lax.fori_loop(0, 4 * len(steps), pair, 0)
    if last:
        for b in range(4):
            o_ref[b] = (acc_ref[b, :, 0:HD] / acc_ref[b, :, HD : 2 * HD]).astype(BF)


def attend(steps, coords, tile_counts, q, blocks, state, last):
    first = state is None
    state_shapes = [
        jax.ShapeDtypeStruct((4, ROWS, 2 * HD), F32),
        jax.ShapeDtypeStruct((4, ROWS, HD), F32),
    ]
    args = [coords, tile_counts, q, *blocks] + ([] if first else list(state))

    def body(*refs):
        attention_body(steps, first, last, *refs)

    specs = [SMEM, SMEM] + [VMEM] * (len(args) - 2)
    held = [pltpu.VMEM((len(steps), ROWS, 2 * HD), BF)] * 2
    if last:
        return call(
            body,
            jax.ShapeDtypeStruct((4, ROWS, HD), BF),
            2.5 * len(steps),
            scratch=[pltpu.VMEM(s.shape, s.dtype) for s in state_shapes] + held,
            in_specs=specs,
        )(*args)
    return call(body, state_shapes, 2.5 * len(steps), scratch=held, in_specs=specs)(*args)


def pack_body(m0, m1, m2, m3, kv_ref, q_ref):
    for k, ref in enumerate((m0, m1, m2, m3)):
        kv_ref[k] = ref[:, 0 : 2 * HD]
        q_ref[k] = ref[:, 2 * HD : 3 * HD]


def turn_body(gain_ref, bias_ref, out_ref):
    out_ref[0:4] = gain_ref[...].T
    out_ref[4:8] = bias_ref[...].T


WINDOW = 896


def window(z):
    return pl.ds(pl.multiple_of(768 * z, HD), WINDOW)


def window_body(w_ref, out_ref):
    for i in range(4):
        out_ref[i] = w_ref[:, 768 * i : 768 * i + WINDOW]


def out_body(s_ref, o0, o1, o2a, o2b, o3, weight, x_any, scale_ref, r_ref, stats_ref, w_ref, x_ref, sems):
    y, z = s_ref[0], s_ref[3]
    copies = [
        pltpu.make_async_copy(weight, w_ref, sems.at[0]),
        pltpu.make_async_copy(x_any.at[:, window(z)], x_ref, sems.at[1]),
    ]
    for copy in copies:
        copy.start()
    acc = jnp.zeros((ROWS, WINDOW), F32)
    for copy in copies:
        copy.wait()
    parts = [
        [o0[k] for k in range(4)],
        [o1[k] for k in range(4)],
        [o2a[0], o2a[1], o2b[0], o2b[1]],
        [o3[k] for k in range(4)],
    ]
    for j in range(4):
        heads = jnp.concatenate(parts[j], axis=1)
        plane = (z - j) & 3
        rows = jnp.concatenate(
            [w_ref[plane, pl.ds(pl.multiple_of(HD * ((y + k) & 3), HD), HD), :] for k in range(4)],
            axis=0,
        )
        acc = acc + cdot(heads, rows)
    residual = cdot(sub_row_permutation(), x_ref[...]) + scale_ref[:, window(z)] * acc
    residual = pltpu.roll(residual, WINDOW - 32 * z, 1)[:, 0 : r_ref.shape[2]]
    total = jnp.zeros((MROWS, 1), F32)
    squares = jnp.zeros((MROWS, 1), F32)
    for sub in range(4):
        part = residual[MROWS * sub : MROWS * (sub + 1)]
        r_ref[sub] = part
        total = total + jnp.sum(part, axis=1, keepdims=True)
        squares = squares + jnp.sum(part * part, axis=1, keepdims=True)
    lane = lax.broadcasted_iota(jnp.int32, (MROWS, HD), 1)
    stats_ref[...] = jnp.where(lane == 0, total, squares)


def merge_body(stats_ref, r_ref, affine_ref, out_ref):
    share = r_ref.shape[2]
    stats = stats_ref[...] * (1.0 / (16 * share))
    mean = stats[:, 0:1]
    scale = lax.rsqrt(stats[:, 1:2] - mean * mean + 1e-05)
    for sub in range(4):
        gain, bias = affine_ref[sub : sub + 1], affine_ref[4 + sub : 5 + sub]
        value = (r_ref[sub] - mean) * scale * gain + bias
        out_ref[:, share * sub : share * (sub + 1)] = value.astype(BF)


def weight_body(s_ref, own_ref, sib_ref, mine_ref, other_ref):
    c = s_ref[2]
    row = lax.broadcasted_iota(jnp.int32, (128, 128), 0)
    col = lax.broadcasted_iota(jnp.int32, (128, 128), 1)
    perm = jnp.where(4 * (row & 31) + (row >> 5) == col, 1.0, 0.0).astype(BF)
    share = own_ref.shape[1] // 4

    def reorder(ref, rows):
        return lax.dot_general(
            perm, ref[:, rows], (((1,), (1,)), ((), ())), preferred_element_type=F32
        ).astype(BF)

    for b in range(own_ref.shape[1] // 128):
        rows = slice(128 * b, 128 * (b + 1))
        own = reorder(own_ref, rows)
        sib = reorder(sib_ref, rows)
        both = jnp.concatenate(
            [jnp.where(c == 0, own, sib), jnp.where(c == 0, sib, own)], axis=1
        )
        for i in range(2):
            dest = slice(share * i + 32 * b, share * i + 32 * (b + 1))
            low = both[32 * i : 32 * (i + 1)]
            high = both[64 + 32 * i : 64 + 32 * (i + 1)]
            mine_ref[dest, :] = jnp.where(c == 0, low, high)
            other_ref[dest, :] = jnp.where(c == 0, high, low)


def projection_body(rels, s_ref, a0, a1, a2a, a2b, a3, mine, other, *refs):
    outs = refs[: len(rels)]
    a_ref, w_ref = refs[len(rels) :]
    x, c, z = s_ref[1], s_ref[2], s_ref[3]
    half = mine.shape[1]

    def rows(j, offset, count):
        return pl.ds(pl.multiple_of(MROWS * ((x - j) & 3) + offset, 16), count)

    a_ref[rows(0, 0, 96), :] = a0[...]
    a_ref[rows(1, 0, 96), :] = a1[...]
    a_ref[rows(2, 0, 48), :] = a2a[...]
    a_ref[rows(2, 48, 48), :] = a2b[...]
    a_ref[rows(3, 0, 96), :] = a3[...]
    for n, rel in enumerate(rels):
        columns = slice(ROWS * n, ROWS * (n + 1))
        k = (z + rel) & 3
        w_ref[pl.ds(pl.multiple_of(half * c, 64), half), columns] = mine[k]
        w_ref[pl.ds(pl.multiple_of(half * (1 - c), 64), half), columns] = other[k]
    acc = cdot(a_ref[...], w_ref[...])
    for n in range(len(rels)):
        outs[n][...] = acc[:, ROWS * n : ROWS * (n + 1)].astype(outs[n].dtype)


def place_body(s_ref, r0, r1, r2a, r2b, r3, slots_ref, text_ref, tslots_ref, own_ref, sib_ref, rows_ref):
    y, x, c = s_ref[0], s_ref[1], s_ref[2]

    def positions(core):
        row = lax.broadcasted_iota(jnp.int32, (448, 1), 0)
        k = (row >= 112).astype(jnp.int32) + (row >= 224).astype(jnp.int32) + (row >= 336).astype(jnp.int32)
        return 112 * (8 * y + 2 * ((x + k) & 3) + core) + row - 112 * k

    def pick(position, slots):
        return jnp.where(position == slots, 1.0, 0.0).astype(BF)

    for k, offset, r in ((0, 0, r0), (1, 0, r1), (2, 0, r2a), (2, 192, r2b), (3, 0, r3)):
        start = pl.multiple_of(ROWS * ((y - k) & 3) + offset, 64)
        rows_ref[pl.ds(start, r.shape[0]), :] = r[...]
    rows = rows_ref[...]
    mine = positions(c)
    own = cdot(pick(mine, slots_ref[...]), rows) + cdot(pick(mine, tslots_ref[...]), text_ref[...])
    own_ref[...] = own.astype(BF)
    sib_ref[...] = cdot(pick(positions(1 - c), slots_ref[...]), rows).astype(BF)


def stream_body(s_ref, b0, b1, b2, b3, out_ref, squares_ref):
    x = s_ref[1]
    width = b0.shape[1]
    total = jnp.zeros((b0.shape[0], 1), F32)
    blocks = [b0[...], b1[...], b2[...], b3[...]]
    for place in range(4):
        k = (x - place) & 3
        value = blocks[0]
        for n in range(1, 4):
            value = jnp.where(k == n, blocks[n], value)
        out_ref[:, width * place : width * (place + 1)] = value
        wide = value.astype(F32)
        total = total + jnp.sum(wide * wide, axis=1, keepdims=True)
    squares_ref[...] = jnp.broadcast_to(total, squares_ref.shape)


def after(values):
    return lax.optimization_barrier(values)


def sum_over_z(value):
    value = value + lax.ppermute(value, "z", [(i, i ^ 1) for i in range(4)])
    return value + lax.ppermute(value, "z", [(i, i ^ 2) for i in range(4)])


def ring(value, axis):
    half = value.shape[0] // 2
    back = shift(value, axis, 1)
    ahead = shift(value, axis, 3)
    return [value, back, shift(back[:half], axis, 1), shift(ahead[half:], axis, 3), ahead]


def per_device(
    patches,
    norm_gain,
    query_weight,
    key_weight,
    value_weight,
    out_weight,
    layer_scale,
    merge_gain,
    merge_bias,
    proj_weight,
    proj_bias,
    text_rows,
    stream_gain,
    tile_counts,
    image_slots,
    text_slots,
):
    y, x, c, z = [lax.axis_index(name).astype(jnp.int32) for name in ("y", "x", "c", "z")]
    coords = jnp.stack([y, x, c, z])
    width = patches.shape[1]
    share = width // 4

    kvq = project_qkv(coords, patches, norm_gain[None], key_weight, value_weight, query_weight)

    turn = [(4 * a + b, 4 * b + a) for a in range(4) for b in range(4)]

    def both_cores(value):
        value = lax.ppermute(value, ("y", "z"), turn)
        sibling = swap(value)
        return jnp.where(
            c == 0,
            jnp.concatenate([value, sibling], axis=1),
            jnp.concatenate([sibling, value], axis=1),
        )

    proj_turned = proj_weight.T
    kvq, out_weight, proj_turned, proj_sibling = after(
        (kvq, out_weight, proj_turned, swap(proj_turned))
    )
    moved = [kvq[0]] + [shift(kvq[k], "y", k) for k in (1, 2, 3)]
    windows = call(
        window_body,
        jax.ShapeDtypeStruct((4, out_weight.shape[0], WINDOW), BF),
        0.1,
        in_specs=[VMEM],
    )(out_weight)
    mine, other = call(
        weight_body,
        (
            jax.ShapeDtypeStruct((2 * share, ROWS), BF),
            jax.ShapeDtypeStruct((2 * share, ROWS), BF),
        ),
        0.1,
        in_specs=[SMEM, VMEM, VMEM],
    )(coords, proj_turned, proj_sibling)
    out_parts = lax.all_to_all(windows, "z", 0, 0, tiled=True)
    gathered = lax.all_gather(mine, "y", axis=0)
    windows, mine, *moved = after((windows, mine, *moved))
    kv_own, q_own = call(
        pack_body,
        (
            jax.ShapeDtypeStruct((4, ROWS, 2 * HD), BF),
            jax.ShapeDtypeStruct((4, ROWS, HD), BF),
        ),
        1,
        in_specs=[VMEM] * 4,
    )(*moved)
    near = [shift(kv_own, "x", 1), shift(kv_own, "x", 3)]
    kv_sib = swap(kv_own)

    where = (coords, tile_counts, q_own)
    state = attend((0,) * 4, *where, [kv_own, kv_sib], None, False)
    near, state = after((near, state))
    far = [shift(near[0][0:2], "x", 1), shift(near[1][2:4], "x", 3)]
    blocks = [near[0], swap(near[0]), near[1], swap(near[1])]
    state = attend((1,) * 4 + (3,) * 4, *where, blocks, state, False)
    far, state, out_parts = after((far, state, out_parts))
    blocks = [far[0], swap(far[0]), far[1], swap(far[1])]
    attended = attend((2,) * 4, *where, blocks, state, True)
    heads = jnp.stack([attended[0]] + [shift(attended[k], "y", 4 - k) for k in (1, 2, 3)])
    gathered, other, heads, merge_gain, merge_bias, layer_scale = after(
        (gathered, other, heads, merge_gain, merge_bias, layer_scale)
    )

    head_parts = ring(heads, "z")
    other_gathered = swap(gathered)
    affine = call(
        turn_body, jax.ShapeDtypeStruct((8, share), F32), 1, in_specs=[VMEM] * 2
    )(merge_gain.reshape(share, 4), merge_bias.reshape(share, 4))
    *head_parts, affine = after((*head_parts, affine))
    residual, stats = call(
        out_body,
        (
            jax.ShapeDtypeStruct((4, MROWS, share), F32),
            jax.ShapeDtypeStruct((MROWS, HD), F32),
        ),
        6,
        scratch=[
            pltpu.VMEM((4, 4 * HD, WINDOW), BF),
            pltpu.VMEM((ROWS, WINDOW), BF),
            pltpu.SemaphoreType.DMA((2,)),
        ],
        in_specs=[SMEM] + [VMEM] * 5 + [ANY] * 2 + [VMEM],
    )(coords, *head_parts, out_parts, patches, layer_scale[None])
    merged = call(
        merge_body, jax.ShapeDtypeStruct((MROWS, width), BF), 1, in_specs=[VMEM] * 3
    )(sum_over_z(stats), residual, affine)

    merged_parts = ring(merged, "x")
    merged, text_rows, proj_bias, image_slots = after((merged, text_rows, proj_bias, image_slots))
    slots = image_slots.reshape(4, 4, 2, MROWS)
    slots = jnp.where(c == 0, slots[:, :, 0], slots[:, :, 1]).reshape(1, 16 * MROWS)
    text = both_cores(text_rows)
    bias_row = both_cores(proj_bias[None])
    *merged_parts, slots, text, bias_row = after((*merged_parts, slots, text, bias_row))

    def project(rels, types):
        return call(
            lambda *refs: projection_body(rels, *refs),
            [jax.ShapeDtypeStruct((ROWS, ROWS), kind) for kind in types],
            5,
            scratch=[pltpu.VMEM((ROWS, width), BF), pltpu.VMEM((width, 2 * ROWS), BF)],
            in_specs=[SMEM] + [VMEM] * 7,
        )(coords, *merged_parts, gathered, other_gathered)

    partial = [None] * 4
    partial[2], partial[1] = project((2, 1), (BF, BF))
    partial[3], summed = project((3, 0), (BF, F32))
    for k in (1, 2, 3):
        summed = summed + shift(partial[k], "z", k).astype(F32)

    rows = jax.nn.gelu(summed + bias_row, approximate=False).astype(BF)

    row_parts = ring(rows, "y")
    placed, for_sibling = call(
        place_body,
        (
            jax.ShapeDtypeStruct((448, ROWS), BF),
            jax.ShapeDtypeStruct((448, ROWS), BF),
        ),
        4,
        scratch=[pltpu.VMEM((4 * ROWS, ROWS), BF)],
        in_specs=[SMEM] + [VMEM] * 8,
    )(coords, *row_parts, slots, text, text_slots[None])
    placed = (placed + swap(for_sibling)).reshape(4, 112, ROWS)
    blocks = [placed[0]] + [shift(placed[k], "x", k) for k in (1, 2, 3)]
    stream, squares = call(
        stream_body,
        (
            jax.ShapeDtypeStruct((112, 4 * ROWS), BF),
            jax.ShapeDtypeStruct((112, HD), F32),
        ),
        2,
        in_specs=[SMEM] + [VMEM] * 4,
    )(coords, *blocks)
    squares = sum_over_z(squares)[:, 0:1]
    inverse_rms = lax.rsqrt(squares * (1.0 / 6144) + 1e-05)
    normed = (stream.astype(F32) * inverse_rms * stream_gain).astype(BF)
    return (stream, normed)


def solution(mesh):
    grid = Mesh(mesh.devices.reshape(4, 4, 2, 4), ("y", "x", "c", "z"))
    seq = ("y", "x", "c")
    return jax.shard_map(
        per_device,
        mesh=grid,
        in_specs=(
            P(seq, None),
            P(),
            P(None, "z"),
            P(None, "z"),
            P(None, "z"),
            P("z", None),
            P(),
            P("z"),
            P("z"),
            P("z", seq),
            P(seq),
            P(None, seq),
            P("z"),
            P(),
            P(),
            P(),
        ),
        out_specs=(P(seq, "z"), P(seq, "z")),
        check_vma=False,
    )
```

time: 356 us -> 292 us (0.82)
  waiting for transfers between devices: 132 us -> 86.7 us
  local copies, waits for them, and re-layouts: 39.3 us -> 16.9 us
  starting transfers between devices: 81 us -> 66.3 us
  between operations: 1.21 us -> 14.5 us
  Pallas kernels: 85.5 us -> 95.9 us
    ppermute x39 -> x28, waiting for transfers between devices: 129 us -> 65 us  [shift(): return lax.ppermute(value, axis, [(i, (i + k) % 4) for i in range(4)])]
    ppermute x39 -> x28, starting transfers between devices: 78.3 us -> 53.9 us  [shift(): return lax.ppermute(value, axis, [(i, (i + k) % 4) for i in range(4)])]
    ppermute x0 -> x4, waiting for transfers between devices: none -> 17.7 us  [the longest x2 9.01 us: sum_over_z(): return value + lax.ppermute(value, 'z', [(i, i ^ 2) for i in range(4)])]
    ppermute x4 -> x0, local copies, waits for them, and re-layouts: 9.29 us -> none  [the longest x3 6.68 us: shift(): return lax.ppermute(value, axis, [(i, (i + k) % 4) for i in range(4)])]
    pallas_call x7 -> x11, Pallas kernels: 73.7 us -> 82.7 us  [the longest x2 27 us: attend(): call(body, state_shapes, 2.5 * len(steps), scratch=held, in_specs=specs)]
    dynamic_slice x5 -> x0, local copies, waits for them, and re-layouts: 7.02 us -> none  [the longest x4 7.01 us: per_device(): lax.dynamic_index_in_dim(columns, z + k & 3, 0, keepdims=False)]
    all_to_all x0 -> x1, starting transfers between devices: none -> 6.57 us  [per_device(): out_parts = lax.all_to_all(windows, 'z', 0, 0, tiled=True)]
    another operation x6 -> x0, local copies, waits for them, and re-layouts: 4.95 us -> none  [the longest x4 2.51 us: per_device(): scalars = jnp.stack([y, x, c, x - k & 3, bounds[0], bounds[1]])]
  transfers between devices with their start and end apart: 52 -> 46, of which waited for: 29 -> 24; matrix products, arithmetic and copies ran while one was open for 11% -> 4% of each run, Pallas kernels for 20% -> 26%
where the time goes in v2:
time: 292 us; the launch traced here: 290 us
  Pallas kernels  95.9 us (33%)
  waiting for transfers between devices  86.7 us (30%)
  starting transfers between devices  66.3 us (23%)
  local copies, waits for them, and re-layouts  16.9 us (6%)
  between operations  14.5 us (5%)
  other arithmetic  9.61 us (3%)
    ppermute x28, waiting for transfers between devices, shift(): return lax.ppermute(value, axis, [(i, (i + k) % 4) for i in range(4)])  65 us
    ppermute x28, starting transfers between devices, shift(): return lax.ppermute(value, axis, [(i, (i + k) % 4) for i in range(4)])  53.9 us
    pallas_call x2, Pallas kernels, attend(): call(body, state_shapes, 2.5 * len(steps), scratch=held, in_specs=specs)  27 us
    pallas_call x2, Pallas kernels, project(): call(lambda *refs: projection_body(rels, *refs), [jax.ShapeDtypeStruct((R...  16.4 us
    pallas_call x1, Pallas kernels, project_qkv(): pl.pallas_call(qkv_body, out_shape=jax.ShapeDtypeStruct((4, ROWS, 3 * HD)...  11.7 us
    pallas_call x1, Pallas kernels, attend(): call(body, jax.ShapeDtypeStruct((4, ROWS, HD), BF), 2.5 * len(steps), scr...  11.4 us
    ppermute x2, waiting for transfers between devices, sum_over_z(): return value + lax.ppermute(value, 'z', [(i, i ^ 2) for i in range(4)])  9.01 us
    unnamed x74, local copies, waits for them, and re-layouts  8.98 us
  transfers between devices with their start and end apart: 46, of which 24 were waited for; matrix products, arithmetic and copies ran while one was open for 4% of the time, Pallas kernels for 26%

profile of v2, /device:TPU:0, one launch (start us, length us, event | category | flops | bytes accessed | tf_op | source)
XLA Modules:
  0.0 289.9 jit_solution(16946904962082520267)
XLA Ops:
  9.2 11.7 %shard_map.167 = bf16[4,384,384]{2,1,0:T(8,128)(2,1)} custom-call(s32[4]{0:T(128)} %pad_add_fusion.s_ref.refs_0_, bf16[384,3200]{1,0:T(8,128)(2,1)} %x_any.1, f32[1,3200]{1,0:T(1,128)} %broadcast_in_dim.13.g_ref, bf16[3200,512]{1,0:T(8,128)(2,1)} %wk_ref.1, bf16[3200,512]{1,0:T(8,128)(2,1)} %wv_ref.1, bf16[3200,512]{1,0:T(8,128)(2,1)} %wq_ref.1), custom_call_target="tpu_custom_call" | custom-call | flops 11000000512 | tf_op jit(solution)/shard_map/pallas_call | solution.py:82
  22.1 5.1 %shard_map.168 = (bf16[1600,384]{1,0:T(8,128)(2,1)}, bf16[1600,384]{1,0:T(8,128)(2,1)}) custom-call(s32[4]{0:T(128)} %pad_add_fusion.s_ref.refs_0_, bf16[192,3200]{1,0:T(8,128)(2,1)} %bitcast.26, bf16[192,3200]{1,0:T(8,128)(2,1)} %copy-done), custom_call_target="tpu_custom_call" | custom-call | flops 100000000 | tf_op jit(solution)/shard_map/pallas_call | solution.py:442
  34.0 4.1 %shard_map.169 = bf16[4,512,896]{2,1,0:T(8,128)(2,1)} custom-call(bf16[512,3200]{1,0:T(8,128)(2,1)} %w_ref), custom_call_target="tpu_custom_call" | custom-call | flops 100000000 | tf_op jit(solution)/shard_map/pallas_call | solution.py:436
  38.8 9.5 %collective-permute-done.2.m2 = bf16[384,384]{1,0:T(8,128)(2,1)S(1)} collective-permute-done((bf16[384,384]{1,0:T(8,128)(2,1)S(1)}, bf16[384,384]{1,0:T(8,128)(2,1)S(1)}, u32[]{:S(2)}, u32[]{:S(2)}) %collective-permute-start.2) | collective-permute-done | bytes 294944 | tf_op jit(solution)/shard_map/ppermute | solution.py:21
  51.5 6.6 %all-to-all-start = ((bf16[4,512,896]{2,1,0:T(8,128)(2,1)}), bf16[4,512,896]{2,1,0:T(8,128)(2,1)}, u32[]{:S(2)}, u32[]{:S(2)}) async-start(bf16[4,512,896]{2,1,0:T(8,128)(2,1)} %shard_map.169), calls=%async_computation | async-start | bytes 7340032 | tf_op jit(solution)/shard_map/all_to_all | solution.py:451
  62.2 9.3 %shard_map.171 = (f32[4,384,256]{2,1,0:T(8,128)}, f32[4,384,128]{2,1,0:T(8,128)}) custom-call(s32[4]{0:T(128)} %pad_add_fusion.s_ref.refs_0_, s32[3]{0:T(128)} %refs_1_.5, bf16[4,384,128]{2,1,0:T(8,128)(2,1)} %get-tuple-element.67.refs_2_, bf16[4,384,256]{2,1,0:T(8,128)(2,1)} %get-tuple-element.68.refs_3_, bf16[4,384,256]{2,1,0:T(8,128)(2,1)} %copy-done.21), custom_call_target="tpu_custom_call" | custom-call | flops 10000000000 | tf_op jit(solution)/shard_map/pallas_call | solution.py:216
  71.5 7.3 %collective-permute-done.4.refs_3_ = bf16[4,384,256]{2,1,0:T(8,128)(2,1)S(1)} collective-permute-done((bf16[4,384,256]{2,1,0:T(8,128)(2,1)S(1)}, bf16[4,384,256]{2,1,0:T(8,128)(2,1)S(1)}, u32[]{:S(2)}, u32[]{:S(2)}) %collective-permute-start.4) | collective-permute-done | bytes 786464 | tf_op jit(solution)/shard_map/ppermute | solution.py:21
  84.6 17.7 %shard_map.172 = (f32[4,384,256]{2,1,0:T(8,128)}, f32[4,384,128]{2,1,0:T(8,128)}) custom-call(s32[4]{0:T(128)} %pad_add_fusion.s_ref.refs_0_, s32[3]{0:T(128)} %refs_1_.5, bf16[4,384,128]{2,1,0:T(8,128)(2,1)} %get-tuple-element.67.refs_2_, bf16[4,384,256]{2,1,0:T(8,128)(2,1)} %copy-done.5, bf16[4,384,256]{2,1,0:T(8,128)(2,1)} %copy-done.20, ...), custom_call_target="tpu_custom_call" | custom-call | flops 20000000000 | tf_op jit(solution)/shard_map/pallas_call | solution.py:216
  106.0 11.4 %shard_map.173 = bf16[4,384,128]{2,1,0:T(8,128)(2,1)} custom-call(s32[4]{0:T(128)} %pad_add_fusion.s_ref.refs_0_, s32[3]{0:T(128)} %refs_1_.5, bf16[4,384,128]{2,1,0:T(8,128)(2,1)} %get-tuple-element.67.refs_2_, bf16[2,384,256]{2,1,0:T(8,128)(2,1)} %collective-permute-done.7.refs_3_, bf16[2,384,256]{2,1,0:T(8,128)(2,1)} %copy-done.22, ...), custom_call_target="tpu_custom_call" | custom-call | flops 10000000000 | tf_op jit(solution)/shard_map/pallas_call | solution.py:209
  133.6 9.6 %collective-permute-done.16.o1 = bf16[4,384,128]{2,1,0:T(8,128)(2,1)S(1)} collective-permute-done((bf16[4,384,128]{2,1,0:T(8,128)(2,1)S(1)}, bf16[4,384,128]{2,1,0:T(8,128)(2,1)S(1)}, u32[]{:S(2)}, u32[]{:S(2)}) %collective-permute-start.16) | collective-permute-done | bytes 393248 | tf_op jit(solution)/shard_map/ppermute | solution.py:21
  153.1 7.3 %shard_map.175 = (f32[4,96,800]{2,1,0:T(8,128)}, f32[96,128]{1,0:T(8,128)}) custom-call(s32[4]{0:T(128)} %pad_add_fusion.s_ref.refs_0_, bf16[4,384,128]{2,1,0:T(8,128)(2,1)} %copy-done.2, bf16[4,384,128]{2,1,0:T(8,128)(2,1)} %copy-done.9, bf16[2,384,128]{2,1,0:T(8,128)(2,1)} %copy-done.29, bf16[2,384,128]{2,1,0:T(8,128)(2,1)} %copy-done.30, ...), custom_call_target="tpu_custom_call" | custom-call | flops 6000000000 | tf_op jit(solution)/shard_map/pallas_call | solution.py:486
  160.5 4.3 %collective-permute-done.20 = f32[96,128]{1,0:T(8,128)S(1)} collective-permute-done((f32[96,128]{1,0:T(8,128)}, f32[96,128]{1,0:T(8,128)S(1)}, u32[]{:S(2)}, u32[]{:S(2)}) %collective-permute-start.20) | collective-permute-done | bytes 49184 | tf_op jit(solution)/shard_map/ppermute | solution.py:384
  166.9 4.3 %collective-permute-done.21 = f32[96,128]{1,0:T(8,128)S(1)} collective-permute-done((f32[96,128]{1,0:T(8,128)S(1)}, f32[96,128]{1,0:T(8,128)S(1)}, u32[]{:S(2)}, u32[]{:S(2)}) %collective-permute-start.21) | collective-permute-done | bytes 49184 | tf_op jit(solution)/shard_map/ppermute | solution.py:385
  174.7 4.2 %collective-permute-start.24 = (bf16[96,3200]{1,0:T(8,128)(2,1)}, bf16[96,3200]{1,0:T(8,128)(2,1)S(1)}, u32[]{:S(2)}, u32[]{:S(2)}) collective-permute-start(bf16[96,3200]{1,0:T(8,128)(2,1)} %shard_map.176.refs_1_), channel_id=1, source_target_pairs={{0,24},{8,0},{16,8},{24,16},{1,25},{9,1},{17,9},{25,17},{2,26},{10... | collective-permute-start | bytes 1843208 | tf_op jit(solution)/shard_map/ppermute | solution.py:21
  181.1 9.0 %collective-permute-done.22.refs_2_ = bf16[96,3200]{1,0:T(8,128)(2,1)S(1)} collective-permute-done((bf16[96,3200]{1,0:T(8,128)(2,1)}, bf16[96,3200]{1,0:T(8,128)(2,1)S(1)}, u32[]{:S(2)}, u32[]{:S(2)}) %collective-permute-start.22) | collective-permute-done | bytes 614432 | tf_op jit(solution)/shard_map/ppermute | solution.py:21
  199.2 8.1 %shard_map.178 = (bf16[384,384]{1,0:T(8,128)(2,1)}, bf16[384,384]{1,0:T(8,128)(2,1)}) custom-call(s32[4]{0:T(128)} %pad_add_fusion.s_ref.refs_0_, bf16[96,3200]{1,0:T(8,128)(2,1)} %shard_map.176.refs_1_, bf16[96,3200]{1,0:T(8,128)(2,1)} %copy-done.7, bf16[48,3200]{1,0:T(8,128)(2,1)} %copy-done.24, bf16[48,3200]{1,0:T(8,128)(2,1)} %copy-done.25, ...), custom_call_target="tpu_custom_call" | custom-call | flops 5000000000 | tf_op jit(solution)/shard_map/pallas_call | solution.py:513
  207.3 4.3 %collective-permute-start.31 = (bf16[384,384]{1,0:T(8,128)(2,1)}, bf16[384,384]{1,0:T(8,128)(2,1)S(1)}, u32[]{:S(2)}, u32[]{:S(2)}) collective-permute-start(bf16[384,384]{1,0:T(8,128)(2,1)} %get-tuple-element.104), channel_id=1, source_target_pairs={{0,1},{1,2},{2,3},{3,0},{4,5},{5,6},{6,7},{7,4},{8,9},{9,10},{10,1... | collective-permute-start | bytes 884744 | tf_op jit(solution)/shard_map/ppermute | solution.py:21
  211.6 5.9 %collective-permute-start.32 = (bf16[384,384]{1,0:T(8,128)(2,1)}, bf16[384,384]{1,0:T(8,128)(2,1)S(1)}, u32[]{:S(2)}, u32[]{:S(2)}) collective-permute-start(bf16[384,384]{1,0:T(8,128)(2,1)} %get-tuple-element.105), channel_id=1, source_target_pairs={{0,2},{1,3},{2,0},{3,1},{4,6},{5,7},{6,4},{7,5},{8,10},{9,11},{10,... | collective-permute-start | bytes 884744 | tf_op jit(solution)/shard_map/ppermute | solution.py:21
  217.6 8.3 %shard_map.177 = (bf16[384,384]{1,0:T(8,128)(2,1)}, f32[384,384]{1,0:T(8,128)}) custom-call(s32[4]{0:T(128)} %pad_add_fusion.s_ref.refs_0_, bf16[96,3200]{1,0:T(8,128)(2,1)} %shard_map.176.refs_1_, bf16[96,3200]{1,0:T(8,128)(2,1)} %copy-done.7, bf16[48,3200]{1,0:T(8,128)(2,1)} %copy-done.24, bf16[48,3200]{1,0:T(8,128)(2,1)} %copy-done.25, ...), custom_call_target="tpu_custom_call" | custom-call | flops 5000000000 | tf_op jit(solution)/shard_map/pallas_call | solution.py:513
  225.8 4.3 %collective-permute-done.32 = bf16[384,384]{1,0:T(8,128)(2,1)S(1)} collective-permute-done((bf16[384,384]{1,0:T(8,128)(2,1)}, bf16[384,384]{1,0:T(8,128)(2,1)S(1)}, u32[]{:S(2)}, u32[]{:S(2)}) %collective-permute-start.32) | collective-permute-done | bytes 294944 | tf_op jit(solution)/shard_map/ppermute | solution.py:21
  239.3 4.7 %collective-permute-done.34.r1 = bf16[384,384]{1,0:T(8,128)(2,1)S(1)} collective-permute-done((bf16[384,384]{1,0:T(8,128)(2,1)S(1)}, bf16[384,384]{1,0:T(8,128)(2,1)S(1)}, u32[]{:S(2)}, u32[]{:S(2)}) %collective-permute-start.34) | collective-permute-done | bytes 294944 | tf_op jit(solution)/shard_map/ppermute | solution.py:21
  251.2 4.0 %shard_map.179 = (bf16[448,384]{1,0:T(8,128)(2,1)}, bf16[448,384]{1,0:T(8,128)(2,1)}) custom-call(s32[4]{0:T(128)} %pad_add_fusion.s_ref.refs_0_, bf16[384,384]{1,0:T(8,128)(2,1)} %copy-done.3, bf16[384,384]{1,0:T(8,128)(2,1)} %copy-done.11, bf16[192,384]{1,0:T(8,128)(2,1)} %copy-done.31, bf16[192,384]{1,0:T(8,128)(2,1)} %copy-done.32, ...), custom_call_target="tpu_custom_call" | custom-call | flops 4000000000 | tf_op jit(solution)/shard_map/pallas_call | solution.py:530
  270.2 4.4 %collective-permute-done.42 = f32[112,128]{1,0:T(8,128)S(1)} collective-permute-done((f32[112,128]{1,0:T(8,128)}, f32[112,128]{1,0:T(8,128)S(1)}, u32[]{:S(2)}, u32[]{:S(2)}) %collective-permute-start.42) | collective-permute-done | bytes 57376 | tf_op jit(solution)/shard_map/ppermute | solution.py:384
  276.3 4.8 %collective-permute-done.43 = f32[112,128]{1,0:T(8,128)S(1)} collective-permute-done((f32[112,128]{1,0:T(8,128)S(1)}, f32[112,128]{1,0:T(8,128)S(1)}, u32[]{:S(2)}, u32[]{:S(2)}) %collective-permute-start.43) | collective-permute-done | bytes 57376 | tf_op jit(solution)/shard_map/ppermute | solution.py:385
  (188 shorter events, 105.3 us)
Async XLA Ops:
  7.2 122.4 %all-gather.3.cloned.1.call-start = ((), (), s32[]{:S(2)}) async-start(), calls=%async_computation.1 | async-start | bytes 6144000 | tf_op jit(solution)/shard_map/all_gather | solution.py:452
  7.2 13.7 %collective-permute-start = (bf16[192,3200]{1,0:T(8,128)(2,1)}, bf16[192,3200]{1,0:T(8,128)(2,1)S(1)}, u32[]{:S(2)}, u32[]{:S(2)}) collective-permute-start(bf16[192,3200]{1,0:T(8,128)(2,1)} %bitcast.25), channel_id=1, source_target_pairs={{0,4},{4,0},{1,5},{5,1},{2,6},{6,2},{3,7},{7,3},{8,12},{12,8},{9,1... | collective-permute-start | bytes 3686408 | tf_op jit(solution)/shard_map/ppermute | solution.py:25
  28.1 10.7 %collective-permute-start.1 = (bf16[384,384]{1,0:T(8,128)(2,1)S(1)}, bf16[384,384]{1,0:T(8,128)(2,1)S(1)}, u32[]{:S(2)}, u32[]{:S(2)}) collective-permute-start(bf16[384,384]{1,0:T(8,128)(2,1)S(1)} %get-tuple-element.116), channel_id=1, source_target_pairs={{0,32},{32,64},{64,96},{96,0},{1,33},{33,65},{65,97},{97,1},{2,34}... | collective-permute-start | bytes 884744 | tf_op jit(solution)/shard_map/ppermute | solution.py:21
  29.8 18.6 %collective-permute-start.2 = (bf16[384,384]{1,0:T(8,128)(2,1)S(1)}, bf16[384,384]{1,0:T(8,128)(2,1)S(1)}, u32[]{:S(2)}, u32[]{:S(2)}) collective-permute-start(bf16[384,384]{1,0:T(8,128)(2,1)S(1)} %get-tuple-element.115), channel_id=1, source_target_pairs={{0,64},{32,96},{64,0},{96,32},{1,65},{33,97},{65,1},{97,33},{2,66}... | collective-permute-start | bytes 884744 | tf_op jit(solution)/shard_map/ppermute | solution.py:21
  32.6 15.7 %collective-permute-start.3 = (bf16[384,384]{1,0:T(8,128)(2,1)S(1)}, bf16[384,384]{1,0:T(8,128)(2,1)S(1)}, u32[]{:S(2)}, u32[]{:S(2)}) collective-permute-start(bf16[384,384]{1,0:T(8,128)(2,1)S(1)} %get-tuple-element.114), channel_id=1, source_target_pairs={{0,96},{32,0},{64,32},{96,64},{1,97},{33,1},{65,33},{97,65},{2,98}... | collective-permute-start | bytes 884744 | tf_op jit(solution)/shard_map/ppermute | solution.py:21
  51.5 9.8 %collective-permute-start.6 = (bf16[4,384,256]{2,1,0:T(8,128)(2,1)}, bf16[4,384,256]{2,1,0:T(8,128)(2,1)S(1)}, u32[]{:S(2)}, u32[]{:S(2)}) collective-permute-start(bf16[4,384,256]{2,1,0:T(8,128)(2,1)} %get-tuple-element.68.refs_3_), channel_id=1, source_target_pairs={{0,4},{4,0},{1,5},{5,1},{2,6},{6,2},{3,7},{7,3},{8,12},{12,8},{9,1... | collective-permute-start | bytes 2359304 | tf_op jit(solution)/shard_map/ppermute | solution.py:25
  51.5 50.9 %all-to-all-start = ((bf16[4,512,896]{2,1,0:T(8,128)(2,1)}), bf16[4,512,896]{2,1,0:T(8,128)(2,1)}, u32[]{:S(2)}, u32[]{:S(2)}) async-start(bf16[4,512,896]{2,1,0:T(8,128)(2,1)} %shard_map.169), calls=%async_computation | async-start | bytes 7340032 | tf_op jit(solution)/shard_map/all_to_all | solution.py:451
  58.1 20.7 %collective-permute-start.4 = (bf16[4,384,256]{2,1,0:T(8,128)(2,1)S(1)}, bf16[4,384,256]{2,1,0:T(8,128)(2,1)S(1)}, u32[]{:S(2)}, u32[]{:S(2)}) collective-permute-start(bf16[4,384,256]{2,1,0:T(8,128)(2,1)S(1)} %copy-done.18), channel_id=1, source_target_pairs={{0,8},{8,16},{16,24},{24,0},{1,9},{9,17},{17,25},{25,1},{2,10},{10... | collective-permute-start | bytes 2359304 | tf_op jit(solution)/shard_map/ppermute | solution.py:21
  59.6 19.2 %collective-permute-start.5 = (bf16[4,384,256]{2,1,0:T(8,128)(2,1)S(1)}, bf16[4,384,256]{2,1,0:T(8,128)(2,1)S(1)}, u32[]{:S(2)}, u32[]{:S(2)}) collective-permute-start(bf16[4,384,256]{2,1,0:T(8,128)(2,1)S(1)} %copy-done.18), channel_id=1, source_target_pairs={{0,24},{8,0},{16,8},{24,16},{1,25},{9,1},{17,9},{25,17},{2,26},{10... | collective-permute-start | bytes 2359304 | tf_op jit(solution)/shard_map/ppermute | solution.py:21
  79.5 22.8 %collective-permute-start.7 = (bf16[2,384,256]{2,1,0:T(8,128)(2,1)S(1)}, bf16[2,384,256]{2,1,0:T(8,128)(2,1)}, u32[]{:S(2)}, u32[]{:S(2)}) collective-permute-start(bf16[2,384,256]{2,1,0:T(8,128)(2,1)S(1)} %slice.77), channel_id=1, source_target_pairs={{0,8},{8,16},{16,24},{24,0},{1,9},{9,17},{17,25},{25,1},{2,10},{10... | collective-permute-start | bytes 1179656 | tf_op jit(solution)/shard_map/ppermute | solution.py:21
  81.0 21.3 %collective-permute-start.8 = (bf16[2,384,256]{2,1,0:T(8,128)(2,1)S(1)}, bf16[2,384,256]{2,1,0:T(8,128)(2,1)}, u32[]{:S(2)}, u32[]{:S(2)}) collective-permute-start(bf16[2,384,256]{2,1,0:T(8,128)(2,1)S(1)} %slice.78), channel_id=1, source_target_pairs={{0,24},{8,0},{16,8},{24,16},{1,25},{9,1},{17,9},{25,17},{2,26},{10... | collective-permute-start | bytes 1179656 | tf_op jit(solution)/shard_map/ppermute | solution.py:21
  129.6 69.0 %collective-permute-start.30 = (bf16[4,1600,384]{2,1,0:T(8,128)(2,1)}, bf16[4,1600,384]{2,1,0:T(8,128)(2,1)}, u32[]{:S(2)}, u32[]{:S(2)}) collective-permute-start(bf16[4,1600,384]{2,1,0:T(8,128)(2,1)} %bitcast.30), channel_id=1, source_target_pairs={{0,4},{4,0},{1,5},{5,1},{2,6},{6,2},{3,7},{7,3},{8,12},{12,8},{9,1... | collective-permute-start | bytes 14745608 | tf_op jit(solution)/shard_map/ppermute | solution.py:25
  129.7 13.6 %collective-permute-start.16 = (bf16[4,384,128]{2,1,0:T(8,128)(2,1)S(1)}, bf16[4,384,128]{2,1,0:T(8,128)(2,1)S(1)}, u32[]{:S(2)}, u32[]{:S(2)}) collective-permute-start(bf16[4,384,128]{2,1,0:T(8,128)(2,1)S(1)} %pad_maximum_fusion.o0), channel_id=1, source_target_pairs={{0,1},{1,2},{2,3},{3,0},{4,5},{5,6},{6,7},{7,4},{8,9},{9,10},{10,1... | collective-permute-start | bytes 1179656 | tf_op jit(solution)/shard_map/ppermute | solution.py:21
  131.5 11.9 %collective-permute-start.18 = (bf16[4,384,128]{2,1,0:T(8,128)(2,1)S(1)}, bf16[4,384,128]{2,1,0:T(8,128)(2,1)S(1)}, u32[]{:S(2)}, u32[]{:S(2)}) collective-permute-start(bf16[4,384,128]{2,1,0:T(8,128)(2,1)S(1)} %pad_maximum_fusion.o0), channel_id=1, source_target_pairs={{0,3},{1,0},{2,1},{3,2},{4,7},{5,4},{6,5},{7,6},{8,11},{9,8},{10,9... | collective-permute-start | bytes 1179656 | tf_op jit(solution)/shard_map/ppermute | solution.py:21
  143.3 8.4 %collective-permute-start.17 = (bf16[2,384,128]{2,1,0:T(8,128)(2,1)S(1)}, bf16[2,384,128]{2,1,0:T(8,128)(2,1)S(1)}, u32[]{:S(2)}, u32[]{:S(2)}) collective-permute-start(bf16[2,384,128]{2,1,0:T(8,128)(2,1)S(1)} %slice.100), channel_id=1, source_target_pairs={{0,1},{1,2},{2,3},{3,0},{4,5},{5,6},{6,7},{7,4},{8,9},{9,10},{10,1... | collective-permute-start | bytes 589832 | tf_op jit(solution)/shard_map/ppermute | solution.py:21
  143.4 8.3 %collective-permute-start.19 = (bf16[2,384,128]{2,1,0:T(8,128)(2,1)S(1)}, bf16[2,384,128]{2,1,0:T(8,128)(2,1)S(1)}, u32[]{:S(2)}, u32[]{:S(2)}) collective-permute-start(bf16[2,384,128]{2,1,0:T(8,128)(2,1)S(1)} %slice.101), channel_id=1, source_target_pairs={{0,3},{1,0},{2,1},{3,2},{4,7},{5,4},{6,5},{7,6},{8,11},{9,8},{10,9... | collective-permute-start | bytes 589832 | tf_op jit(solution)/shard_map/ppermute | solution.py:21
  174.4 15.7 %collective-permute-start.22 = (bf16[96,3200]{1,0:T(8,128)(2,1)}, bf16[96,3200]{1,0:T(8,128)(2,1)S(1)}, u32[]{:S(2)}, u32[]{:S(2)}) collective-permute-start(bf16[96,3200]{1,0:T(8,128)(2,1)} %shard_map.176.refs_1_), channel_id=1, source_target_pairs={{0,8},{8,16},{16,24},{24,0},{1,9},{9,17},{17,25},{25,1},{2,10},{10... | collective-permute-start | bytes 1843208 | tf_op jit(solution)/shard_map/ppermute | solution.py:21
  174.7 16.3 %collective-permute-start.24 = (bf16[96,3200]{1,0:T(8,128)(2,1)}, bf16[96,3200]{1,0:T(8,128)(2,1)S(1)}, u32[]{:S(2)}, u32[]{:S(2)}) collective-permute-start(bf16[96,3200]{1,0:T(8,128)(2,1)} %shard_map.176.refs_1_), channel_id=1, source_target_pairs={{0,24},{8,0},{16,8},{24,16},{1,25},{9,1},{17,9},{25,17},{2,26},{10... | collective-permute-start | bytes 1843208 | tf_op jit(solution)/shard_map/ppermute | solution.py:21
  180.5 14.0 %collective-permute-start.29 = (f32[1,192]{1,0:T(1,128)S(1)}, f32[1,192]{1,0:T(1,128)S(1)}, u32[]{:S(2)}, u32[]{:S(2)}) collective-permute-start(f32[1,192]{1,0:T(1,128)S(1)} %collective-permute-done.28), channel_id=1, source_target_pairs={{0,4},{4,0},{1,5},{5,1},{2,6},{6,2},{3,7},{7,3},{8,12},{12,8},{9,1... | collective-permute-start | bytes 2312 | tf_op jit(solution)/shard_map/ppermute | solution.py:25
  180.6 13.9 %collective-permute-start.27 = (bf16[512,192]{1,0:T(8,128)(2,1)S(1)}, bf16[512,192]{1,0:T(8,128)(2,1)S(1)}, u32[]{:S(2)}, u32[]{:S(2)}) collective-permute-start(bf16[512,192]{1,0:T(8,128)(2,1)S(1)} %collective-permute-done.26), channel_id=1, source_target_pairs={{0,4},{4,0},{1,5},{5,1},{2,6},{6,2},{3,7},{7,3},{8,12},{12,8},{9,1... | collective-permute-start | bytes 589832 | tf_op jit(solution)/shard_map/ppermute | solution.py:25
  190.2 8.1 %collective-permute-start.23 = (bf16[48,3200]{1,0:T(8,128)(2,1)S(1)}, bf16[48,3200]{1,0:T(8,128)(2,1)S(1)}, u32[]{:S(2)}, u32[]{:S(2)}) collective-permute-start(bf16[48,3200]{1,0:T(8,128)(2,1)S(1)} %slice.102), channel_id=1, source_target_pairs={{0,8},{8,16},{16,24},{24,0},{1,9},{9,17},{17,25},{25,1},{2,10},{10... | collective-permute-start | bytes 921608 | tf_op jit(solution)/shard_map/ppermute | solution.py:21
  207.3 18.5 %collective-permute-start.31 = (bf16[384,384]{1,0:T(8,128)(2,1)}, bf16[384,384]{1,0:T(8,128)(2,1)S(1)}, u32[]{:S(2)}, u32[]{:S(2)}) collective-permute-start(bf16[384,384]{1,0:T(8,128)(2,1)} %get-tuple-element.104), channel_id=1, source_target_pairs={{0,1},{1,2},{2,3},{3,0},{4,5},{5,6},{6,7},{7,4},{8,9},{9,10},{10,1... | collective-permute-start | bytes 884744 | tf_op jit(solution)/shard_map/ppermute | solution.py:21
  211.6 18.5 %collective-permute-start.32 = (bf16[384,384]{1,0:T(8,128)(2,1)}, bf16[384,384]{1,0:T(8,128)(2,1)S(1)}, u32[]{:S(2)}, u32[]{:S(2)}) collective-permute-start(bf16[384,384]{1,0:T(8,128)(2,1)} %get-tuple-element.105), channel_id=1, source_target_pairs={{0,2},{1,3},{2,0},{3,1},{4,6},{5,7},{6,4},{7,5},{8,10},{9,11},{10,... | collective-permute-start | bytes 884744 | tf_op jit(solution)/shard_map/ppermute | solution.py:21
  259.1 8.4 %collective-permute-start.40 = (bf16[112,384]{1,0:T(8,128)(2,1)S(1)}, bf16[112,384]{1,0:T(8,128)(2,1)S(1)}, u32[]{:S(2)}, u32[]{:S(2)}) collective-permute-start(bf16[112,384]{1,0:T(8,128)(2,1)S(1)} %get-tuple-element.123), channel_id=1, source_target_pairs={{0,16},{8,24},{16,0},{24,8},{1,17},{9,25},{17,1},{25,9},{2,18},{10... | collective-permute-start | bytes 258056 | tf_op jit(solution)/shard_map/ppermute | solution.py:21
  (59 other events, 417.5 us)
Sparse Core Ops, SparseCore 0:
  27.4 58.8 all-gather.2
